TPU v7x, 32 devices: a whole 2x2x4 slice. The times are simulated.
32 devices in a mesh: tile: 8 (over z, x), anc: 4 (over y, core).
Axes of the slice: x: 2, y: 2, z: 4, core: 2. Of those that a mesh axis runs over, the one named last changes fastest.
Arguments:
- points: bfloat16 [7, 35, 60416], P(None, None, ('tile', 'anc')), may hold values from -6 to 6
- npoints: int32 [60416], P(('tile', 'anc')), may hold values from 1 to 35
- coords: int32 [60416, 3], P(('tile', 'anc')), may hold values from 0 to 383, as said below
- labels: int32 [2, 384, 352], P(None, ('tile', 'anc')), may hold values from 0 to 2
- targets: float32 [2, 7, 384, 352], P(None, None, ('tile', 'anc')), may hold values from -6 to 6
- w_vfe1: bfloat16 [7, 32], replicated, may hold values from -2 to 2
- w_vfe2: bfloat16 [64, 128], replicated, may hold values from -0.75 to 0.75
- w_mid: bfloat16 [3, 3, 3, 128, 64], replicated, may hold values from -0.25 to 0.25
- w_rpn: bfloat16 [3, 3, 320, 128], P(None, None, 'anc'), may hold values from -0.15625 to 0.15625
- w_head: bfloat16 [128, 16], replicated, may hold values from -0.5 to 0.5
- bn_gain: bfloat16 [32], replicated, may hold values from 0.5 to 1.5
- biases: bfloat16 [368], replicated, may hold values from -0.59765625 to 0.59765625
- master: float32 [600688], P('anc'), may hold values from -0.18 to 0.18
- moment1: float32 [600688], P('anc'), may hold values from -4.3004195e-05 to 4.3004195e-05
- moment2: float32 [600688], P('anc'), may hold values from 4.1618944e-12 to 1.6647577e-11
Outputs:
- master_new: float32 [600688], P('anc')
- moment1_new: float32 [600688], P('anc')
- moment2_new: float32 [600688], P('anc')
- loss: float32 [], replicated
- grad_norm: float32 [], replicated
Inputs may be any that keep to these rules, and one draw needn't show every extreme that they name: `coords`: every voxel occupies its own cell. The voxels of each block of 7552 consecutive voxels lie in the same 48 map rows, block t in rows t * 48 to (t+1) * 48 - 1.
All inputs are finite; a program needn't handle non-finite values.
Results may differ from a plain program's by a relative error of at most 0.0023.
Values may be sent and summed in bfloat16 or wider, within the bound.
No kernel may reach another device: no remote copies, remote signals or barrier semaphores. Data moves between devices by JAX's collectives and lax.ppermute only.
A program may use at most 256 MiB of HBM per device.

v0:
```python
import jax
import jax.numpy as jnp
from jax import lax
from jax.sharding import PartitionSpec as P

DEPTH = 10
ANCH = 2
SCENE_TILES = 4
TR = 48


PRECISE = lax.Precision.HIGHEST
FOCAL_ALPHA = 0.25
BN_EPSILON = 0.001
CLIP_LIMIT = 0.05
LEARN_RATE = 0.03
BETA_FIRST = 0.9
BETA_SECOND = 0.999
WEIGHT_DECAY = 0.01
ADAM_EPSILON = 1e-08
STEP_NUMBER = 10


def extended(shard, sides, width):
    for axis, dim in sides:
        count, length = (lax.axis_size(axis), shard.shape[dim])
        up = [(i, (i + 1) % count) for i in range(count - 1)]
        down = [(j, i) for i, j in up]
        last = lax.slice_in_dim(shard, length - width, length, axis=dim)
        first = lax.slice_in_dim(shard, 0, width, axis=dim)
        before = lax.ppermute(last, axis, up)
        after = lax.ppermute(first, axis, down)
        shard = jnp.concatenate([before, shard, after], axis=dim)
    return shard


def detection(heads, labels, targets):
    logits = heads[:, 0]
    boxes = heads[:, 1:]
    probab = jax.nn.sigmoid(logits)
    positive = (labels == 1).astype(jnp.float32)
    negative = (labels == 0).astype(jnp.float32)
    focal = positive * FOCAL_ALPHA * (1.0 - probab) ** 2 * jax.nn.softplus(-logits)
    focal = focal + negative * (1.0 - FOCAL_ALPHA) * probab**2 * jax.nn.softplus(logits)
    offset = boxes - targets
    magnitude = jnp.abs(offset)
    smooth = jnp.where(magnitude < 1.0 / 9.0, 4.5 * offset * offset, magnitude - 1.0 / 18.0)
    return jnp.sum(focal) + 2.0 * jnp.sum(smooth * positive[:, None])


def plane_conv(padded, kernel):
    return lax.conv_general_dilated(
        padded[None],
        kernel,
        (1, 1),
        "VALID",
        dimension_numbers=("NHWC", "HWIO", "NHWC"),
        preferred_element_type=jnp.float32,
    )[0]


def pool_back(acts, pooled, grads):
    ties = (acts == pooled[:, None, :]).astype(jnp.float32)
    return ties * (grads / jnp.sum(ties, axis=1))[:, None, :]


def scene_edges(padded, dim, tile_index, tile_rows):
    length = padded.shape[dim]
    place = lax.broadcasted_iota(jnp.int32, (length,), 0)
    crop_rows = SCENE_TILES * TR
    half_crop = crop_rows // 2
    first_row = tile_index * tile_rows
    lower_cut = first_row % crop_rows == half_crop
    upper_cut = (first_row + tile_rows) % crop_rows == half_crop
    cut = (place == 0) & lower_cut | (place == length - 1) & upper_cut
    shape = [1] * padded.ndim
    shape[dim] = length
    return padded * jnp.logical_not(cut).reshape(shape).astype(padded.dtype)


def place_grid(feats, crd, tile_index, tile_rows, columns):
    return (
        jnp.zeros((DEPTH, tile_rows, columns, feats.shape[1]), jnp.bfloat16)
        .at[crd[:, 0], crd[:, 1] - tile_index * tile_rows, crd[:, 2]]
        .set(feats)
    )


def on_device(
    points,
    npoints,
    coords,
    labels,
    targets,
    w_vfe1,
    w_vfe2,
    w_mid,
    w_rpn,
    w_head,
    bn_gain,
    biases,
    master,
    moment1,
    moment2,
):
    anc_count = lax.axis_size("anc")
    anc_index = lax.axis_index("anc")
    tile_index = lax.axis_index("tile")
    quarter_rows = labels.shape[1]
    columns = labels.shape[2]
    tile_rows = quarter_rows * anc_count
    c_vfe = w_vfe1.shape[1]
    c_vox = w_vfe2.shape[1]
    c_mid = w_mid.shape[4]
    c_rpn = w_rpn.shape[3]
    depth_out = DEPTH // 2
    mid_part = c_mid // anc_count
    bias_all = biases.astype(jnp.float32)
    shift = bias_all[:c_vfe]
    bias_two = bias_all[c_vfe : c_vfe + c_vox]
    bias_mid = bias_all[c_vfe + c_vox : c_vfe + c_vox + c_mid]
    bias_rpn = bias_all[c_vfe + c_vox + c_mid : c_vfe + c_vox + c_mid + c_rpn]
    bias_head = bias_all[c_vfe + c_vox + c_mid + c_rpn :]
    gain = bn_gain.astype(jnp.float32)
    slots = points.shape[1]
    voxels = points.shape[2]
    validity = (lax.broadcasted_iota(jnp.int32, (slots, voxels), 0) < npoints[None, :]).astype(
        jnp.float32
    )
    hidden_one = jnp.einsum("kpv,kc->cpv", points, w_vfe1, preferred_element_type=jnp.float32)
    positives = jnp.sum((labels == 1).astype(jnp.float32))
    total_first, total_second, count_all, count_pos = lax.psum(
        (
            jnp.sum(hidden_one * validity, axis=(1, 2)),
            jnp.sum(hidden_one * hidden_one * validity, axis=(1, 2)),
            jnp.sum(validity),
            positives,
        ),
        ("tile", "anc"),
    )
    average = total_first / count_all
    variance = total_second / count_all - average * average
    inv_std = lax.rsqrt(variance + BN_EPSILON)
    normed = (hidden_one - average[:, None, None]) * inv_std[:, None, None]
    affine = gain[:, None, None] * normed + shift[:, None, None]
    act_one = jax.nn.relu(affine) * validity
    pooled_one = jnp.max(act_one, axis=1)
    joined = jnp.concatenate(
        [act_one, jnp.broadcast_to(pooled_one[:, None, :], act_one.shape)], axis=0
    ).astype(jnp.bfloat16)
    pre_two = (
        jnp.einsum("cpv,co->opv", joined, w_vfe2, preferred_element_type=jnp.float32)
        + bias_two[:, None, None]
    )
    act_two = jax.nn.relu(pre_two) * validity
    pooled_two = jnp.max(act_two, axis=1)
    features = pooled_two.T.astype(jnp.bfloat16)
    layer_index = coords[:, 0]
    row_local = coords[:, 1] - tile_index * tile_rows
    column_index = coords[:, 2]
    voxel_grid = place_grid(features, coords, tile_index, tile_rows, columns)
    grid_rim = scene_edges(extended(voxel_grid, (("tile", 1),), 1), 1, tile_index, tile_rows)
    middle_out = lax.conv_general_dilated(
        grid_rim[None],
        w_mid,
        (2, 1, 1),
        ((1, 0), (0, 0), (1, 1)),
        dimension_numbers=("NDHWC", "DHWIO", "NDHWC"),
        preferred_element_type=jnp.float32,
    )[0]
    middle_bev = jnp.transpose(middle_out, (1, 2, 3, 0)).reshape(tile_rows, columns, -1)
    bev_sums = lax.psum_scatter(middle_bev, "anc", scatter_dimension=2, tiled=True)
    bias_part = jnp.repeat(
        lax.dynamic_slice_in_dim(bias_mid, anc_index * mid_part, mid_part), depth_out
    )
    pre_mid = bev_sums + bias_part
    bev = jax.nn.relu(pre_mid).astype(jnp.bfloat16)
    bev_rim = scene_edges(extended(bev, (("tile", 0),), 1), 0, tile_index, tile_rows)
    bev_padded = jnp.pad(bev_rim, ((0, 0), (1, 1), (0, 0)))
    pre_rpn = (
        lax.psum_scatter(plane_conv(bev_padded, w_rpn), "anc", scatter_dimension=0, tiled=True)
        + bias_rpn
    )
    rpn_act = jax.nn.relu(pre_rpn).astype(jnp.bfloat16)
    heads = (
        jnp.einsum("rcx,xh->hrc", rpn_act, w_head, preferred_element_type=jnp.float32)
        + bias_head[:, None, None]
    )
    heads_grouped = heads.reshape(ANCH, -1, quarter_rows, columns)
    numerator, pullback = jax.vjp(
        lambda output_heads: detection(output_heads, labels, targets), heads_grouped
    )
    d_heads = pullback(jnp.ones((), jnp.float32) / count_pos)[0].reshape(heads.shape)
    grad_head = jnp.einsum("rcx,hrc->xh", rpn_act.astype(jnp.float32), d_heads, precision=PRECISE)
    grad_bias_head = jnp.sum(d_heads, axis=(1, 2))
    d_rpn_act = jnp.einsum("hrc,xh->rcx", d_heads, w_head.astype(jnp.float32), precision=PRECISE)
    d_pre_rpn = (d_rpn_act * (pre_rpn > 0)).astype(jnp.bfloat16)
    grad_bias_rpn = jnp.sum(d_pre_rpn.astype(jnp.float32), axis=(0, 1))
    d_rows = lax.all_gather(d_pre_rpn, "anc", axis=0, tiled=True)
    d_rows_rim = scene_edges(extended(d_rows, (("tile", 0),), 1), 0, tile_index, tile_rows)
    d_rows_padded = jnp.pad(d_rows_rim, ((0, 0), (1, 1), (0, 0)))
    flipped = jnp.transpose(w_rpn[::-1, ::-1], (0, 1, 3, 2))
    d_bev = plane_conv(d_rows_padded, flipped)
    grad_rpn = jnp.stack(
        [
            jnp.einsum(
                "rci,rco->io",
                bev_padded[row_off : row_off + tile_rows, col_off : col_off + columns],
                d_rows,
                preferred_element_type=jnp.float32,
            )
            for row_off in range(3)
            for col_off in range(3)
        ]
    ).reshape(3, 3, -1, c_rpn)
    d_pre_mid = (d_bev * (pre_mid > 0)).astype(jnp.bfloat16)
    bias_mid_part = jnp.sum(
        jnp.sum(d_pre_mid.astype(jnp.float32), axis=(0, 1)).reshape(mid_part, depth_out), axis=1
    )
    grad_bias_mid = lax.dynamic_update_slice(
        jnp.zeros((c_mid,), jnp.float32), bias_mid_part, (anc_index * mid_part,)
    )
    d_mid_all = lax.all_gather(
        d_pre_mid.reshape(tile_rows, columns, mid_part, depth_out), "anc", axis=2, tiled=True
    )
    d_mid_depth = jnp.transpose(d_mid_all, (3, 0, 1, 2))
    d_mid_rim = scene_edges(extended(d_mid_depth, (("tile", 1),), 1), 1, tile_index, tile_rows)
    d_mid_table = jnp.pad(d_mid_rim, ((0, 0), (0, 0), (1, 1), (0, 0))).reshape(-1, c_mid)
    offsets = lax.broadcasted_iota(jnp.int32, (27, 1), 0)
    depth_off = offsets // 9
    row_off = offsets // 3 % 3
    col_off = offsets % 3
    shifted = layer_index[None, :] + 1 - depth_off
    usable = (shifted % 2 == 0) & (shifted >= 0) & (shifted <= 2 * depth_out - 2)
    out_depth = jnp.clip(shifted // 2, 0, depth_out - 1)
    gather_index = (
        (out_depth * (tile_rows + 2) + row_local[None, :] - row_off + 2) * (columns + 2)
        + column_index[None, :]
        - col_off
        + 2
    )
    picked = d_mid_table[gather_index] * usable[:, :, None].astype(jnp.bfloat16)
    kernel_flat = w_mid.reshape(27, c_vox, c_mid)
    d_features = jnp.einsum("kvo,kio->vi", picked, kernel_flat, preferred_element_type=jnp.float32)
    grad_mid = jnp.einsum("vi,kvo->kio", features, picked, preferred_element_type=jnp.float32)
    d_act_two = pool_back(act_two, pooled_two, d_features.T)
    d_pre_two = (d_act_two * (pre_two > 0) * validity).astype(jnp.bfloat16)
    grad_bias_two = jnp.sum(d_pre_two.astype(jnp.float32), axis=(1, 2))
    grad_two = jnp.einsum("cpv,opv->co", joined, d_pre_two, preferred_element_type=jnp.float32)
    d_joined = jnp.einsum("opv,co->cpv", d_pre_two, w_vfe2, preferred_element_type=jnp.float32)
    d_act_one = d_joined[:c_vfe] + pool_back(act_one, pooled_one, jnp.sum(d_joined[c_vfe:], axis=1))
    d_affine = d_act_one * (affine > 0) * validity
    local_shift = jnp.sum(d_affine, axis=(1, 2))
    local_gain = jnp.sum(d_affine * normed, axis=(1, 2))
    total_shift, total_gain, loss_total = lax.psum(
        (local_shift, local_gain, numerator), ("tile", "anc")
    )
    d_hidden_one = (
        (gain * inv_std)[:, None, None]
        * (d_affine - (total_shift[:, None, None] + normed * total_gain[:, None, None]) / count_all)
        * validity
    ).astype(jnp.bfloat16)
    grad_one = jnp.einsum("kpv,cpv->kc", points, d_hidden_one, preferred_element_type=jnp.float32)
    block_length = grad_rpn.size
    rpn_blocks = lax.dynamic_update_slice(
        jnp.zeros((anc_count, block_length), jnp.float32), grad_rpn.reshape(1, -1), (anc_index, 0)
    )
    flattened = jnp.concatenate(
        [
            rpn_blocks.reshape(-1),
            grad_one.reshape(-1),
            grad_two.reshape(-1),
            grad_mid.reshape(-1),
            grad_head.reshape(-1),
            local_gain,
            local_shift,
            grad_bias_two,
            grad_bias_mid,
            grad_bias_rpn,
            grad_bias_head,
        ]
    )
    share_sum = lax.psum_scatter(flattened, "anc", scatter_dimension=0, tiled=True)
    reduced = lax.psum(share_sum, "tile")
    square_sum = lax.psum(jnp.sum(reduced * reduced), "anc")
    norm_value = jnp.sqrt(square_sum)
    clipped = reduced * jnp.minimum(1.0, CLIP_LIMIT / (norm_value + 1e-06))
    first = BETA_FIRST * moment1 + (1.0 - BETA_FIRST) * clipped
    second = BETA_SECOND * moment2 + (1.0 - BETA_SECOND) * clipped * clipped
    first_hat = first / (1.0 - BETA_FIRST**STEP_NUMBER)
    second_hat = second / (1.0 - BETA_SECOND**STEP_NUMBER)
    updated = master - LEARN_RATE * (
        first_hat / (jnp.sqrt(second_hat) + ADAM_EPSILON) + WEIGHT_DECAY * master
    )
    return (updated, first, second, loss_total / count_pos, norm_value)


def solution(mesh):
    placed = (
        P(None, None, ("tile", "anc")),
        P(("tile", "anc")),
        P(("tile", "anc"), None),
        P(None, ("tile", "anc"), None),
        P(None, None, ("tile", "anc"), None),
        P(),
        P(),
        P(),
        P(None, None, "anc", None),
        P(),
        P(),
        P(),
        P("anc"),
        P("anc"),
        P("anc"),
    )
    return jax.shard_map(
        on_device,
        mesh=mesh,
        in_specs=placed,
        out_specs=(P("anc"), P("anc"), P("anc"), P(), P()),
        check_vma=False,
    )
```

profile of v0, /device:TPU:0, one launch (start us, length us, event | category | flops | bytes accessed | tf_op | source)
XLA Modules:
  0.0 1849.9 jit_solution(12843210744851517868)
XLA Ops:
  21.2 42.3 %all-reduce.7 = (f32[32]{0:T(128)S(1)}, f32[]{:T(128)}, f32[32]{0:T(128)S(1)}) all-reduce(f32[32]{0:T(128)S(1)} %get-tuple-element.14, f32[]{:T(128)} %fusion.151, f32[32]{0:T(128)S(1)} %get-tuple-element.13), channel_id=1, replica_groups=mesh['tile'=8,'anc'=4] {'tile','anc'}, use_global_device_ids=true, to_apply=%region_1.0 | all-reduce | flops 65 | bytes 520 | tf_op jit(solution)/shard_map/psum | solution.py:132
  76.9 17.9 bitcast_reduce_fusion
  95.8 13.9 broadcast.541
  109.7 187.1 %scatter_fusion = bf16[168960,128]{1,0:T(8,128)(2,1)} fusion(bf16[168960,128]{1,0:T(8,128)(2,1)} %broadcast.541, s32[1888]{0:T(1024)S(1)} %broadcast_select_fusion.4, bf16[1888,128]{1,0:T(8,128)(2,1)S(1)} %convert_bitcast_fusion), kind=kCustom, calls=%fused_computation.1 | custom fusion | bytes 1457536
  305.0 34.7 %collective-permute-done = bf16[10,1,352,128]{3,2,0,1:T(8,128)(2,1)} collective-permute-done((bf16[10,1,352,128]{3,2,0,1:T(8,128)(2,1)S(1)}, bf16[10,1,352,128]{3,2,0,1:T(8,128)(2,1)}, u32[]{:S(2)}, u32[]{:S(2)}) %collective-permute-start) | collective-permute-done | bytes 901152 | tf_op jit(solution)/shard_map/ppermute | solution.py:31
  339.7 30.6 %fusion.8 = bf16[10,50,1,352,128]{4,3,1,0,2:T(8,128)(2,1)} fusion(bf16[1,10,1,352,128]{4,3,2,1,0:T(8,128)(2,1)} %bitcast.7, bf16[1,10,48,352,128]{4,3,2,1,0:T(8,128)(2,1)} %bitcast.233, bf16[1,10,1,352,128]{4,3,2,1,0:T(8,128)(2,1)} %bitcast.5, bf16[50]{0:T(256)(128)(2,1)S(1)} %not_convert_fusion), kind=kLoop, calls=%fused_computation.11 | loop fusion | flops 67584000 | bytes 90112096 | tf_op jit(solution)/shard_map/mul | solution.py:78
  370.3 30.5 %pad.23 = bf16[10,50,1,360,128]{4,3,1,0,2:T(8,128)(2,1)} pad(bf16[10,50,1,352,128]{4,3,1,0,2:T(8,128)(2,1)} %fusion.8, bf16[]{:T(256)} %constant.156.clone.1), padding=0_0x0_0x0_0x1_7x0_0 | pad | bytes 91136000 | tf_op jit(solution)/shard_map/mul | solution.py:78
  400.8 63.9 %reshape.511 = bf16[10,50,1,8,45,128]{5,4,3,1,0,2:T(8,128)(2,1)} reshape(bf16[10,50,1,360,128]{4,3,1,0,2:T(8,128)(2,1)} %pad.23) | data formatting | bytes 92160000 | tf_op jit(solution)/shard_map/conv_general_dilated | solution.py:163
  464.7 32.0 %copy.60 = bf16[10,50,1,8,45,128]{5,3,4,1,0,2:T(8,128)(2,1)} copy(bf16[10,50,1,8,45,128]{5,4,3,1,0,2:T(8,128)(2,1)} %reshape.511) | data formatting | bytes 92160000 | tf_op jit(solution)/shard_map/conv_general_dilated | solution.py:163
  498.8 181.9 %broadcast_select_fusion = f32[5,48,8,45,64]{4,2,3,1,0:T(8,128)} fusion(pred[8,45]{0,1:T(8,128)(4,1)S(1)} %copy-done.58, bf16[3,3,3,128,64]{3,4,2,1,0:T(8,128)(2,1)} %param.23, bf16[10,50,1,7,2,128]{5,3,4,1,0,2:T(8,128)(2,1)S(1)} %slice.135, bf16[10,50,1,8,45,128]{5,3,4,1,0,2:T(8,128)(2,1)} %copy.60), kind=kOutput, calls=%fused_computation.20 | convolution fusion | flops 35822469120 | bytes 70433128 | tf_op jit(solution)/shard_map/conv_general_dilated | solution.py:163
  680.7 36.0 %copy.61 = f32[5,48,8,45,64]{4,1,3,2,0:T(8,128)} copy(f32[5,48,8,45,64]{4,2,3,1,0:T(8,128)} %broadcast_select_fusion) | data formatting | bytes 44236800 | tf_op jit(solution)/shard_map/conv_general_dilated | solution.py:163
  716.8 28.6 %slice_bitcast_fusion = f32[48,352,64,5]{2,0,1,3:T(8,128)} fusion(f32[5,48,1,360,64]{4,1,3,0,2:T(8,128)} %bitcast.234), kind=kLoop, calls=%fused_computation.12 | loop fusion | bytes 43253760 | tf_op jit(solution)/shard_map/transpose | solution.py:171
  745.4 42.4 %copy.62 = f32[48,352,64,5]{1,0,3,2:T(8,128)} copy(f32[48,352,64,5]{2,0,1,3:T(8,128)} %slice_bitcast_fusion) | data formatting | bytes 43253760 | tf_op jit(solution)/shard_map/transpose | solution.py:171
  787.7 20.1 %copy.63 = f32[48,352,320]{1,2,0:T(8,128)} copy(f32[48,352,320]{1,0,2:T(8,128)} %bitcast.235) | data formatting | bytes 43253760 | tf_op jit(solution)/shard_map/reshape | solution.py:171
  808.8 170.4 %reduce-scatter.3.cloned.1.call-done = f32[48,352,80]{1,2,0:T(8,128)} async-done(((f32[48,352,320]{1,2,0:T(8,128)}), f32[48,352,80]{1,2,0:T(8,128)}) %reduce-scatter.3.cloned.1.call-update) | async-done | bytes 5406736 | tf_op jit(solution)/shard_map/reduce_scatter | solution.py:172
  998.7 11.8 reshape.583
  1022.5 13.7 broadcast_select_fusion.2
  1045.3 72.7 %reduce-scatter.5.cloned.1.call-done = f32[12,352,128]{2,1,0:T(8,128)} async-done(((f32[48,352,128]{2,1,0:T(8,128)}), f32[12,352,128]{2,1,0:T(8,128)}) %reduce-scatter.5.cloned.1.call-update) | async-done | bytes 2162704 | tf_op jit(solution)/shard_map/reduce_scatter | solution.py:181
  1121.0 39.5 %psum.66 = f32[]{:T(128)} all-reduce(f32[]{:T(128)} %get-tuple-element.18), channel_id=1, replica_groups=mesh['tile'=8,'anc'=4] {'tile','anc'}, use_global_device_ids=true, to_apply=%region_12.13 | all-reduce | flops 1 | bytes 8 | tf_op jit(solution)/shard_map/psum | solution.py:132
  1168.3 36.3 %all-gather.3.cloned.1.call-done = bf16[48,352,128]{2,1,0:T(8,128)(2,1)} async-done(((bf16[12,352,128]{2,1,0:T(8,128)(2,1)}), bf16[48,352,128]{2,1,0:T(8,128)(2,1)}) %all-gather.3.cloned.1.call-update) | async-done | bytes 4325392 | tf_op jit(solution)/shard_map/all_gather | solution.py:199
  1271.1 21.0 %convert_reduce_fusion.1 = f32[128,1888]{0,1:T(8,128)} fusion(f32[35,1888,128]{2,1,0:T(8,128)} %get-tuple-element.62, f32[128,1888]{0,1:T(8,128)} %copy-done.6, f32[35,1888]{1,0:T(8,128)S(1)} %copy-done.5, f32[128]{0:T(128)} %copy-done.40), kind=kLoop, calls=%fused_computation.17 | loop fusion | flops 50507776 | bytes 36031104 | tf_op jit(solution)/shard_map/reduce_sum | solution.py:64
  1318.7 20.8 %all-gather.5.cloned.1.call-done = bf16[48,352,64,5]{1,0,3,2:T(8,128)(2,1)} async-done(((bf16[48,352,16,5]{1,0,3,2:T(8,128)(2,1)}), bf16[48,352,64,5]{1,0,3,2:T(8,128)(2,1)}) %all-gather.5.cloned.1.call-update) | async-done | bytes 10813456 | tf_op jit(solution)/shard_map/all_gather | solution.py:223
  1388.3 15.0 reshape.497
  1403.4 20.9 %copy.76 = bf16[88500,64]{1,0:T(8,128)(2,1)} copy(bf16[88500,64]{0,1:T(8,128)(2,1)} %reshape.497) | data formatting | bytes 22656000 | tf_op jit(solution)/shard_map/reshape | solution.py:228
  1424.3 104.9 %gather_fusion = bf16[50976,64]{1,0:T(8,128)(2,1)} fusion(bf16[88500,64]{1,0:T(8,128)(2,1)} %copy.76, s32[51200]{0:T(1024)S(1)} %copy-done.15), kind=kCustom, calls=%fused_computation | custom fusion | bytes 13253760 | tf_op jit(solution)/shard_map/gather | solution.py:242
  1529.2 13.8 copy.77
  1551.1 24.3 %convert_reduce_fusion = (f32[128]{0:T(128)}, bf16[128,35,1888]{0,2,1:T(8,128)(2,1)}) fusion(f32[35,1888]{1,0:T(8,128)S(1)} %copy-done.5, f32[128,1888]{0,1:T(8,128)S(1)} %fusion.61, f32[128,1888]{0,1:T(8,128)S(1)} %copy-done.7, f32[35,1888,128]{2,1,0:T(8,128)} %get-tuple-element.62, f32[128]{0:T(128)S(1)} %copy-done.41), kind=kLoop, calls=%fused_computation.15 | loop fusion | flops 93040512 | bytes 52948096 | tf_op jit(solution)/shard_map/reduce_sum | solution.py:248
  1583.8 17.6 convolution_bitcast_fusion
  1620.9 41.5 %all-reduce.6 = (f32[32]{0:T(128)S(1)}, f32[32]{0:T(128)S(1)}, f32[]{:T(128)}) all-reduce(f32[32]{0:T(128)} %get-tuple-element.16, f32[32]{0:T(128)S(1)} %get-tuple-element.15, f32[]{:T(128)S(6)} %add.354), channel_id=1, replica_groups=mesh['tile'=8,'anc'=4] {'tile','anc'}, use_global_device_ids=true, to_apply=%region_19.21 | all-reduce | flops 65 | bytes 520 | tf_op jit(solution)/shard_map/psum | solution.py:255
  1670.8 22.7 %concatenate.44 = f32[600688]{0:T(1024)} concatenate(f32[368640]{0:T(1024)S(1)} %bitcast.243, f32[224]{0:T(256)S(1)} %reshape.499, f32[8192]{0:T(1024)S(1)} %copy-done.26, f32[221184]{0:T(1024)} %reshape.501, f32[2048]{0:T(1024)S(1)} %copy-done.27, f32[32]{0:T(128)S(1)} %copy-done.47, f32[32]{0:T(128)S(1)} %get-tuple-element.15, f32[128]{0:T(128)S(1)} %copy-done.49, ...), dimensions={0} | concatenate | bytes 4805504 | tf_op jit(solution)/shard_map/concatenate | solution.py:268
  1694.9 55.4 %all-reduce.13.cloned.1.call-done = f32[600688]{0:T(1024)} async-done(((f32[600688]{0:T(1024)}), f32[600688]{0:T(1024)}) %all-reduce.13.cloned.1.call-update) | async-done | bytes 2402768
  1752.5 74.8 %all-reduce.11.cloned.1.call-done = f32[150172]{0:T(1024)} async-done(((f32[150172]{0:T(1024)}), f32[150172]{0:T(1024)}) %all-reduce.11.cloned.1.call-update) | async-done | bytes 600704 | tf_op jit(solution)/shard_map/psum | solution.py:284
  (260 shorter events, 288.5 us)
Async XLA Ops:
  7.2 56.3 %copy-start.54 = (bf16[32]{0:T(256)(128)(2,1)S(1)}, bf16[32]{0:T(256)(128)(2,1)}, u32[]{:S(2)}) copy-start(bf16[32]{0:T(256)(128)(2,1)} %param.26) | copy-start | bytes 196
  7.2 972.1 %reduce-scatter.3.cloned.1.call-start = ((), (), s32[]{:S(2)}) async-start(), calls=%async_computation.2 | async-start | bytes 29491200 | tf_op jit(solution)/shard_map/reduce_scatter | solution.py:172
  8.0 64.6 %copy-start.42 = (f32[32]{0:T(128)}, f32[32]{0:T(128)S(1)}, u32[]{:S(2)}) copy-start(f32[32]{0:T(128)S(1)} %slice.98) | copy-start | bytes 388
  9.3 67.5 %copy-start.40 = (f32[128]{0:T(128)}, f32[128]{0:T(128)S(1)}, u32[]{:S(2)}) copy-start(f32[128]{0:T(128)S(1)} %get-tuple-element.59) | copy-start | bytes 1540
  11.4 65.4 %copy-start.4 = (f32[35,1888]{1,0:T(8,128)}, f32[35,1888]{1,0:T(8,128)S(1)}, u32[]{:S(2)}) copy-start(f32[35,1888]{1,0:T(8,128)S(1)} %fusion.120) | copy-start | bytes 792964
  12.2 60.4 %copy-start.44 = (f32[32]{0:T(128)}, f32[32]{0:T(128)S(1)}, u32[]{:S(2)}) copy-start(f32[32]{0:T(128)S(1)} %convert_element_type.94) | copy-start | bytes 388
  298.4 41.3 %collective-permute-start = (bf16[10,1,352,128]{3,2,0,1:T(8,128)(2,1)S(1)}, bf16[10,1,352,128]{3,2,0,1:T(8,128)(2,1)}, u32[]{:S(2)}, u32[]{:S(2)}) collective-permute-start(bf16[10,1,352,128]{3,2,0,1:T(8,128)(2,1)S(1)} %get-tuple-element.43), channel_id=1, source_target_pairs={{0,4},{4,8},{8,12},{12,16},{16,20},{20,24},{24,28},{1,5},{5,9},{9,... | collective-permute-start | bytes 2703368 | tf_op jit(solution)/shard_map/ppermute | solution.py:31
  303.7 36.0 %collective-permute-start.1 = (bf16[10,1,352,128]{3,2,0,1:T(8,128)(2,1)S(1)}, bf16[10,1,352,128]{3,2,0,1:T(8,128)(2,1)}, u32[]{:S(2)}, u32[]{:S(2)}) collective-permute-start(bf16[10,1,352,128]{3,2,0,1:T(8,128)(2,1)S(1)} %get-tuple-element.44), channel_id=1, source_target_pairs={{4,0},{8,4},{12,8},{16,12},{20,16},{24,20},{28,24},{5,1},{9,5},{13... | collective-permute-start | bytes 2703368 | tf_op jit(solution)/shard_map/ppermute | solution.py:32
  305.0 65.3 %copy-start.34 = (bf16[50]{0:T(256)(128)(2,1)}, bf16[50]{0:T(256)(128)(2,1)S(1)}, u32[]{:S(2)}) copy-start(bf16[50]{0:T(256)(128)(2,1)S(1)} %not_convert_fusion) | copy-start | bytes 304
  464.7 34.1 %copy-start.58 = (pred[8,45]{0,1:T(8,128)(4,1)S(1)}, pred[8,45]{0,1:T(8,128)(4,1)}, u32[]{:S(2)}) copy-start(pred[8,45]{0,1:T(8,128)(4,1)} %constant.228) | copy-start | bytes 1084
  807.8 184.2 %copy-start.35 = (bf16[50]{0:T(256)(128)(2,1)S(1)}, bf16[50]{0:T(256)(128)(2,1)}, u32[]{:S(2)}) copy-start(bf16[50]{0:T(256)(128)(2,1)} %copy-done.34) | copy-start | bytes 304
  807.8 310.2 %reduce-scatter.5.cloned.1.call-start = ((), (), s32[]{:S(2)}) async-start(), calls=%async_computation.3 | async-start | bytes 10813440 | tf_op jit(solution)/shard_map/reduce_scatter | solution.py:181
  982.6 5.2 collective-permute-start.2
  986.0 6.1 collective-permute-start.3
  1044.5 73.5 %copy-start.32 = (bf16[128,16]{0,1:T(8,128)(2,1)S(1)}, bf16[128,16]{0,1:T(8,128)(2,1)}, u32[]{:S(2)}) copy-start(bf16[128,16]{0,1:T(8,128)(2,1)} %param.25) | copy-start | bytes 12292
  1044.5 73.5 %copy-start.33 = (f32[128]{0:T(128)S(1)}, f32[128]{0:T(128)}, u32[]{:S(2)}) copy-start(f32[128]{0:T(128)} %get-tuple-element.58) | copy-start | bytes 1540
  1044.5 117.1 %copy-start.22 = (f32[2,7,12,352]{3,0,2,1:T(2,128)S(1)}, f32[2,7,12,352]{3,0,2,1:T(2,128)}, u32[]{:S(2)}) copy-start(f32[2,7,12,352]{3,0,2,1:T(2,128)} %param.20) | copy-start | bytes 709636
  1044.6 160.0 %all-gather.3.cloned.1.call-start = ((), (), s32[]{:S(2)}) async-start(), calls=%async_computation.4 | async-start | bytes 5406720 | tf_op jit(solution)/shard_map/all_gather | solution.py:199
  1168.3 171.2 %all-gather.5.cloned.1.call-start = ((), (), s32[]{:S(2)}) async-start(), calls=%async_computation.5 | async-start | bytes 14745600 | tf_op jit(solution)/shard_map/all_gather | solution.py:223
  1205.5 5.7 collective-permute-start.4
  1208.9 6.4 collective-permute-start.5
  1261.7 488.7 %all-reduce.13.cloned.1.call-start = ((), (), s32[]{:S(2)}) async-start(), calls=%async_computation.7 | async-start | bytes 4808704
  1271.1 24.6 %copy-start.3 = (f32[12,352,128]{2,1,0:T(8,128)S(1)}, f32[12,352,128]{2,1,0:T(8,128)}, u32[]{:S(2)}) copy-start(f32[12,352,128]{2,1,0:T(8,128)} %reduce-scatter.5.cloned.1.call-done) | copy-start | bytes 6488068
  1343.3 25.2 %collective-permute-start.6 = (bf16[5,1,352,64]{2,1,0,3:T(2,128)(2,1)}, bf16[5,1,352,64]{2,1,0,3:T(2,128)(2,1)S(1)}, u32[]{:S(2)}, u32[]{:S(2)}) collective-permute-start(bf16[5,1,352,64]{2,1,0,3:T(2,128)(2,1)} %get-tuple-element.45), channel_id=1, source_target_pairs={{0,4},{4,8},{8,12},{12,16},{16,20},{20,24},{24,28},{1,5},{5,9},{9,... | collective-permute-start | bytes 675848 | tf_op jit(solution)/shard_map/ppermute | solution.py:31
  1346.8 21.7 %collective-permute-start.7 = (bf16[5,1,352,64]{2,1,0,3:T(2,128)(2,1)}, bf16[5,1,352,64]{2,1,0,3:T(2,128)(2,1)}, u32[]{:S(2)}, u32[]{:S(2)}) collective-permute-start(bf16[5,1,352,64]{2,1,0,3:T(2,128)(2,1)} %get-tuple-element.46), channel_id=1, source_target_pairs={{4,0},{8,4},{12,8},{16,12},{20,16},{24,20},{28,24},{5,1},{9,5},{13... | collective-permute-start | bytes 675848 | tf_op jit(solution)/shard_map/ppermute | solution.py:32
  1548.9 26.5 %slice-start.2 = ((s8[4300800]{0:T(1024)(128)(4,1)}), s8[4194304]{0:T(1024)(128)(4,1)S(1)}, s32[]{:S(2)}) async-start(s8[4300800]{0:T(1024)(128)(4,1)} %bitcast.245), calls=%async_computation.10 | async-start | bytes 8388608
  1549.0 26.5 %slice-start.4 = ((s8[4300800]{0:T(1024)(128)(4,1)}), s8[4194304]{0:T(1024)(128)(4,1)S(1)}, s32[]{:S(2)}) async-start(s8[4300800]{0:T(1024)(128)(4,1)} %bitcast.247), calls=%async_computation.12 | async-start | bytes 8388608
  1551.1 24.4 %slice-start.3 = ((s8[4300800]{0:T(1024)(128)(4,1)}), s8[106496]{0:T(1024)(128)(4,1)S(1)}, s32[]{:S(2)}) async-start(s8[4300800]{0:T(1024)(128)(4,1)} %bitcast.245), calls=%async_computation.11 | async-start | bytes 212992
  1551.1 24.4 %slice-start.5 = ((s8[4300800]{0:T(1024)(128)(4,1)}), s8[106496]{0:T(1024)(128)(4,1)S(1)}, s32[]{:S(2)}) async-start(s8[4300800]{0:T(1024)(128)(4,1)} %bitcast.247), calls=%async_computation.13 | async-start | bytes 212992
  1670.7 23.0 %copy-start.57 = (u32[32]{0:T(128)S(1)}, u32[32]{0:T(128)}, u32[]{:S(2)}) copy-start(u32[32]{0:T(128)} %constant.234) | copy-start | bytes 388
  1670.7 166.7 %copy-start.19 = (f32[150172]{0:T(1024)S(1)}, f32[150172]{0:T(1024)}, u32[]{:S(2)}) copy-start(f32[150172]{0:T(1024)} %param.28) | copy-start | bytes 1802068
  1693.6 133.7 %all-reduce.11.cloned.1.call-start = ((), (), s32[]{:S(2)}) async-start(), calls=%async_computation.6 | async-start | bytes 1204224 | tf_op jit(solution)/shard_map/psum | solution.py:284
  (47 other events, 359.8 us)
Sparse Core Ops, SparseCore 0:
  808.0 171.2 reduce-scatter.2
  1044.7 73.2 reduce-scatter.4
  1168.4 36.1 all-gather.2
  1261.8 77.6 all-gather.4
  1693.7 56.5 all-reduce.12
  1754.2 73.0 all-reduce.10
where the time goes:
time: 1870 us; the launch traced here: 1850 us
  local copies, waits for them, and re-layouts  741 us (40%)
  waiting for transfers between devices  480 us (26%)
  matrix products  305 us (16%)
  other arithmetic  151 us (8%)
  blocking collectives  130 us (7%)
  between operations  22.3 us (1%)
  starting transfers between devices  20.9 us (1%)
    unnamed x138, local copies, waits for them, and re-layouts  224 us
    conv_general_dilated x1, matrix products, on_device(): lax.conv_general_dilated(grid_rim[None], w_mid, (2, 1, 1), ((1, 0), (0, 0...  182 us
    reduce_scatter x1, waiting for transfers between devices, on_device(): lax.psum_scatter(middle_bev, 'anc', scatter_dimension=2, tiled=True)  170 us
    conv_general_dilated x4, local copies, waits for them, and re-layouts, on_device(): lax.conv_general_dilated(grid_rim[None], w_mid, (2, 1, 1), ((1, 0), (0, 0...  134 us
    gather x2, local copies, waits for them, and re-layouts, on_device(): picked = d_mid_table[gather_index] * usable[:, :, None].astype(jnp.bfloat16)  119 us
    psum x2, blocking collectives, on_device(): lax.psum((jnp.sum(hidden_one * validity, axis=(1, 2)), jnp.sum(hidden_one...  81.8 us
    psum x1, waiting for transfers between devices, on_device(): reduced = lax.psum(share_sum, 'tile')  74.8 us
    reduce_scatter x1, waiting for transfers between devices, on_device(): lax.psum_scatter(plane_conv(bev_padded, w_rpn), 'anc', scatter_dimension=...  72.7 us
  transfers between devices with their start and end apart: 14, of which 12 were waited for; matrix products, arithmetic and copies ran while one was open for 4% of the time, Pallas kernels for 0%

commit v1 on v0

v1 whole, which is shorter than its diff:
```python
import functools
import jax
import jax.numpy as jnp
from jax import lax
from jax.experimental import pallas as pl
from jax.experimental.pallas import tpu as pltpu
from jax.sharding import PartitionSpec as P

DEPTH = 10
PAIRS = DEPTH // 4 + 1
CROP_ROWS = 192
BLOCK_ROWS = 12
HALO = 2
LANES = 128
CHUNK = 384
CAP = 768
EDGE_CAP = 128
LARGE_ROWS = 2304
FOCAL_ALPHA = 0.25
BN_EPSILON = 0.001
CLIP_LIMIT = 0.05
LEARN_RATE = 0.03
BETA_FIRST = 0.9
BETA_SECOND = 0.999
WEIGHT_DECAY = 0.01
ADAM_EPSILON = 1e-08
STEP_NUMBER = 10
F32 = jnp.float32
BF16 = jnp.bfloat16
VMEM_LIMIT = 60 * 1024 * 1024


def vmem(count):
    return [pl.BlockSpec(memory_space=pltpu.VMEM)] * count


def smem(count):
    return [pl.BlockSpec(memory_space=pltpu.SMEM)] * count


def params(*semantics):
    return pltpu.CompilerParams(vmem_limit_bytes=VMEM_LIMIT, dimension_semantics=semantics or None)


def work(micros):
    return pl.CostEstimate(flops=micros, transcendentals=0, bytes_accessed=micros * 3_000_000)


def at_row(index, columns):
    return pl.ds(pl.multiple_of(index * columns, 32), columns)


def column_edges(columns, lanes):
    place = lax.broadcasted_iota(jnp.int32, (columns, lanes), 0)
    return place == 0, place == columns - 1


def from_left(values):
    columns, lanes = values.shape
    first, _ = column_edges(columns, lanes)
    return jnp.where(first, 0.0, pltpu.roll(values, 1, 0))


def from_right(values):
    columns, lanes = values.shape
    _, last = column_edges(columns, lanes)
    return jnp.where(last, 0.0, pltpu.roll(values, columns - 1, 0))


def low_lanes(columns):
    return lax.broadcasted_iota(jnp.int32, (columns, LANES), 1) < LANES // 2


def scatter_kernel(count, cells, fresh, *refs):
    if fresh:
        index_ref, feat_ref, out_ref, wide, rows = refs
    else:
        index_ref, feat_ref, old_ref, out_ref, wide, rows = refs
    step = 512

    def begin(i, carry):
        block = pl.ds(pl.multiple_of(i * step, step), step)
        if fresh:
            wide[block, :] = jnp.zeros((step, LANES), F32)
        else:
            wide[block, :] = old_ref[block, :].astype(F32)
        return carry

    lax.fori_loop(0, cells // step, begin, 0)
    rows[...] = feat_ref[...].astype(F32)

    def place(i, carry):
        for j in range(8):
            wide[pl.ds(index_ref[i * 8 + j], 1), :] = rows[pl.ds(i * 8 + j, 1), :]
        return carry

    lax.fori_loop(0, count // 8, place, 0)

    def finish(i, carry):
        block = pl.ds(pl.multiple_of(i * step, step), step)
        out_ref[block, :] = wide[block, :].astype(BF16)
        return carry

    lax.fori_loop(0, cells // step, finish, 0)


def scatter_rows(index, feats, old, columns):
    cells = DEPTH * (BLOCK_ROWS + 2 * HALO) * columns
    count = index.shape[0]
    fresh = old is None
    return pl.pallas_call(
        functools.partial(scatter_kernel, count, cells, fresh),
        out_shape=jax.ShapeDtypeStruct((cells, LANES), BF16),
        in_specs=smem(1) + vmem(1 if fresh else 2),
        out_specs=vmem(1)[0],
        scratch_shapes=[pltpu.VMEM((cells + 8, LANES), F32), pltpu.VMEM((count, LANES), F32)],
        compiler_params=params(),
        cost_estimate=work(15),
        name="grid_scatter",
    )(*((index, feats) if fresh else (index, feats, old)))


def middle_kernel(columns, edge_ref, grid_ref, weight_ref, bias_ref, out_ref):
    low = low_lanes(columns)
    grid_rows = BLOCK_ROWS + 2 * HALO
    depth_out = DEPTH // 2

    def row(m, carry):
        sums = []
        for o in range(depth_out):
            taps = (1, 2) if o == 0 else (0, 1, 2)
            left = jnp.concatenate(
                [
                    grid_ref[at_row((2 * o + a - 1) * grid_rows + m + b, columns), :]
                    for a in taps
                    for b in range(3)
                ],
                axis=1,
            )
            right = weight_ref[o % 2, 3 * LANES * (3 - len(taps)) :, :]
            sums.append(jnp.dot(left, right, preferred_element_type=F32))
        inside = (m > 0) & (m < BLOCK_ROWS + 1) | (m == 0) & (edge_ref[0] > 0)
        inside = inside | (m == BLOCK_ROWS + 1) & (edge_ref[1] > 0)
        keep = jnp.where(inside, 1.0, 0.0)
        for j in range(PAIRS):
            even = sums[2 * j]
            if 2 * j + 1 < depth_out:
                odd = sums[2 * j + 1]
                first = jnp.where(low, even[:, :LANES], odd[:, :LANES])
                middle = jnp.where(low, odd[:, :LANES], even[:, :LANES])
                last = even[:, LANES:] + odd[:, LANES:]
            else:
                first = even[:, :LANES]
                middle = first
                last = even[:, LANES:]
            total = from_left(first) + pltpu.roll(middle, LANES // 2, 1) + from_right(last)
            total = jnp.maximum(total + bias_ref[0:1, :], 0.0) * keep
            if 2 * j + 1 == depth_out:
                total = jnp.where(low, total, 0.0)
            out_ref[at_row(m, columns), j * LANES : (j + 1) * LANES] = total.astype(BF16)
        return carry

    lax.fori_loop(0, BLOCK_ROWS + 2, row, 0)


def middle_weights(w_mid):
    c_mid = w_mid.shape[4]
    kernel = w_mid.transpose(0, 1, 3, 2, 4).reshape(-1, 3, c_mid)
    none = jnp.zeros_like(kernel[:, 0])
    even = jnp.concatenate([kernel[:, 0], kernel[:, 1], kernel[:, 2], none], axis=1)
    odd = jnp.concatenate([kernel[:, 1], kernel[:, 0], none, kernel[:, 2]], axis=1)
    return jnp.stack([even, odd])


def middle_forward(edges, grid, weights, bias, columns):
    return pl.pallas_call(
        functools.partial(middle_kernel, columns),
        out_shape=jax.ShapeDtypeStruct(((BLOCK_ROWS + 2) * columns, PAIRS * LANES), BF16),
        in_specs=smem(1) + vmem(3),
        out_specs=vmem(1)[0],
        compiler_params=params(),
        cost_estimate=work(26),
        name="middle_forward",
    )(edges, grid, weights, jnp.tile(bias.reshape(1, -1), (8, 2)))


def column_taps(own, j):
    low = low_lanes(own.shape[0])
    other = pltpu.roll(own, LANES // 2, 1)
    both = [jnp.where(low, own, other)]
    if 2 * j + 1 < DEPTH // 2:
        both.append(jnp.where(low, other, own))
    return [(jnp.where(low, from_right(x), x), from_left(x)) for x in both]


def middle_data_kernel(
    count, columns, index_ref, edge_ref, d_ref, above_ref, below_ref, weight_ref, out_ref,
    near, far, wide, rows,
):
    padded = BLOCK_ROWS + 2
    half = LANES // 2
    cells = DEPTH * BLOCK_ROWS * columns

    def build(r, source, place, factor):
        for j in range(PAIRS):
            own = source[place, j * LANES : (j + 1) * LANES].astype(F32)
            if factor is not None:
                own = jnp.where(factor > 0, own, 0.0)
            for k, (pair, left) in enumerate(column_taps(own, j)):
                o = 2 * j + k
                near[o, at_row(r, columns), :] = pair.astype(BF16)
                far[o, at_row(r, columns), 0:half] = left[:, 0:half].astype(BF16)
                if not (isinstance(r, int) and r == 0):
                    far[o, at_row(r - 1, columns), half:LANES] = left[:, half:].astype(BF16)

    def build_own(r, carry):
        build(r + 1, d_ref, at_row(r, columns), None)
        return carry

    whole = slice(0, columns)
    build(0, above_ref, whole, edge_ref[0])
    lax.fori_loop(0, BLOCK_ROWS, build_own, 0)
    build(BLOCK_ROWS + 1, below_ref, whole, edge_ref[1])
    for o in range(DEPTH // 2):
        far[o, (padded - 1) * columns :, half:LANES] = jnp.zeros((columns, half), BF16)

    def row(r, carry):
        def pieces(o):
            return [near[o, at_row(r + i, columns), :] for i in range(3)] + [
                far[o, at_row(r + i, columns), :] for i in (0, 2)
            ]

        for o in range(DEPTH // 2):
            left = jnp.concatenate(pieces(o) + (pieces(o + 1) if o < DEPTH // 2 - 1 else []), axis=1)
            total = jnp.dot(left, weight_ref[0 : left.shape[1], :], preferred_element_type=F32)
            wide[at_row(2 * o * BLOCK_ROWS + r, columns), :] = total[:, :LANES]
            wide[at_row((2 * o + 1) * BLOCK_ROWS + r, columns), :] = total[:, LANES:]
        return carry

    lax.fori_loop(0, BLOCK_ROWS, row, 0)
    wide[cells:, :] = jnp.zeros((8, LANES), F32)

    def pick(i, carry):
        for j in range(8):
            rows[pl.ds(i * 8 + j, 1), :] = wide[pl.ds(index_ref[i * 8 + j], 1), :]
        return carry

    lax.fori_loop(0, count // 8, pick, 0)
    out_ref[...] = rows[...].astype(BF16)


def middle_data_weights(w_mid):
    three, _, _, c_in, c_out = w_mid.shape
    turned = w_mid.transpose(0, 1, 2, 4, 3)[:, ::-1]
    near = turned[:, :, :2].reshape(three, -1, c_in)
    far = turned[:, :, 2].reshape(three, -1, c_in)
    block = jnp.concatenate([near, far, jnp.zeros((three, c_out, c_in), w_mid.dtype)], axis=1)
    none = jnp.zeros_like(block[0])
    return jnp.concatenate(
        [
            jnp.concatenate([block[1], none], axis=0),
            jnp.concatenate([block[2], block[0]], axis=0),
        ],
        axis=1,
    )


def middle_data(index, edges, d_rows, above, below, weights, columns):
    count = index.shape[0]
    padded = (BLOCK_ROWS + 2) * columns
    return pl.pallas_call(
        functools.partial(middle_data_kernel, count, columns),
        out_shape=jax.ShapeDtypeStruct((count, LANES), BF16),
        in_specs=smem(2) + vmem(4),
        out_specs=vmem(1)[0],
        scratch_shapes=[
            pltpu.VMEM((DEPTH // 2, padded, LANES), BF16),
            pltpu.VMEM((DEPTH // 2, padded, LANES), BF16),
            pltpu.VMEM((DEPTH * BLOCK_ROWS * columns + 8, LANES), F32),
            pltpu.VMEM((count, LANES), F32),
        ],
        compiler_params=params(),
        cost_estimate=work(30),
        name="middle_data",
    )(index, edges, d_rows, above, below, weights)


def middle_weight_kernel(columns, grid_ref, d_ref, out_ref, total, taps_ref, turned):
    grid_rows = BLOCK_ROWS + 2 * HALO
    half = LANES // 2
    total[...] = jnp.zeros_like(total)

    def rows(i, carry):
        for k in range(2):
            for j in range(PAIRS):
                own = d_ref[at_row(i * 2 + k, columns), j * LANES : (j + 1) * LANES].astype(F32)
                for n, (pair, left) in enumerate(column_taps(own, j)):
                    place = slice(k * columns, (k + 1) * columns)
                    taps_ref[2 * j + n, place, 0:LANES] = pair.astype(BF16)
                    taps_ref[2 * j + n, place, LANES:] = left.astype(BF16)
        for o in range(DEPTH // 2):
            depth_taps = (1, 2) if o == 0 else (0, 1, 2)
            cells = jnp.concatenate(
                [
                    grid_ref[
                        pl.ds(
                            pl.multiple_of(
                                ((2 * o + a - 1) * grid_rows + i * 2 + 1 + b) * columns, 32
                            ),
                            2 * columns,
                        ),
                        :,
                    ]
                    for a in depth_taps
                    for b in range(3)
                ],
                axis=1,
            )
            part = lax.dot_general(
                taps_ref[o], cells, (((0,), (0,)), ((), ())), preferred_element_type=F32
            )
            if o == 0:
                total[:, 3 * LANES :] += part
            else:
                total[...] += part
        return carry

    lax.fori_loop(0, BLOCK_ROWS // 2, rows, 0)
    low = low_lanes(LANES // 2)
    used = 27 * half
    out_ref[used:, :] = jnp.zeros((out_ref.shape[0] - used, LANES), F32)
    for place in range(9):
        for side in range(2):
            turned[...] = total[
                side * LANES : (side + 1) * LANES, place * LANES : (place + 1) * LANES
            ].T
            even = turned[pl.ds(0, half, stride=2), :]
            odd = turned[pl.ds(1, half, stride=2), :]
            at = (place * 3 + side * 2) * half
            out_ref[at : at + half, :] = jnp.where(low, even, pltpu.roll(odd, half, 1))
            if side == 0:
                out_ref[at + half : at + 2 * half, :] = jnp.where(
                    low, pltpu.roll(even, half, 1), odd
                )


def middle_weight(grid, d_rows, columns, total_rows):
    return pl.pallas_call(
        functools.partial(middle_weight_kernel, columns),
        out_shape=jax.ShapeDtypeStruct((total_rows, LANES), F32),
        in_specs=vmem(2),
        out_specs=vmem(1)[0],
        scratch_shapes=[
            pltpu.VMEM((2 * LANES, 9 * LANES), F32),
            pltpu.VMEM((DEPTH // 2, 2 * columns, 2 * LANES), BF16),
            pltpu.VMEM((LANES, LANES), F32),
        ],
        compiler_params=params(),
        cost_estimate=work(26),
        name="middle_weight",
    )(grid, d_rows)


def region_kernel(
    columns,
    scale_ref,
    bev_ref,
    weight_ref,
    bias_ref,
    head_ref,
    head_bias_ref,
    labels_ref,
    targets_ref,
    d_ref,
    first_ref,
    last_ref,
    grad_head_ref,
    sums_ref,
    head_sum,
    loss_sum,
):
    width = PAIRS * LANES
    outs = head_ref.shape[0]
    scale = scale_ref[0, 0]
    head = head_ref[...]
    head_three = jnp.concatenate([head, head, head], axis=0)
    grad_head_ref[...] = jnp.zeros_like(grad_head_ref)
    sums_ref[...] = jnp.zeros_like(sums_ref)
    head_sum[...] = jnp.zeros_like(head_sum)
    loss_sum[...] = jnp.zeros_like(loss_sum)
    kind = lax.broadcasted_iota(jnp.int32, (outs, columns), 0) % 8 == 0

    def row(r, carry):
        left = jnp.concatenate([bev_ref[at_row(r + b, columns), :] for b in range(3)], axis=1)
        part = jnp.dot(left, weight_ref[...], preferred_element_type=F32)
        pre = from_left(part[:, :LANES]) + part[:, LANES : 2 * LANES]
        pre = pre + from_right(part[:, 2 * LANES :]) + bias_ref[0:1, :]
        act = jnp.maximum(pre, 0.0).astype(BF16)
        heads = lax.dot_general(head, act, (((1,), (1,)), ((), ())), preferred_element_type=F32)
        heads = heads + head_bias_ref[:, 0:1]
        label = labels_ref[r]
        positive = jnp.where(label == 1, 1.0, 0.0)
        negative = jnp.where(label == 0, 1.0, 0.0)
        tail = jnp.log1p(jnp.exp(-jnp.abs(heads)))
        soft_up = jnp.maximum(heads, 0.0) + tail
        soft_down = jnp.maximum(-heads, 0.0) + tail
        probab = jax.nn.sigmoid(heads)
        rest = 1.0 - probab
        focal = positive * FOCAL_ALPHA * rest * rest * soft_down
        focal = focal + negative * (1.0 - FOCAL_ALPHA) * probab * probab * soft_up
        d_focal = positive * FOCAL_ALPHA * rest * rest * (-2.0 * probab * soft_down - rest)
        d_focal = d_focal + negative * (1.0 - FOCAL_ALPHA) * probab * probab * (
            2.0 * rest * soft_up + probab
        )
        offset = heads - targets_ref[r]
        size = jnp.abs(offset)
        near = size < 1.0 / 9.0
        smooth = jnp.where(near, 4.5 * offset * offset, size - 1.0 / 18.0)
        d_smooth = jnp.where(near, 9.0 * offset, jnp.where(offset > 0.0, 1.0, -1.0))
        loss_sum[...] += jnp.where(kind, focal, 2.0 * positive * smooth)
        d_heads = jnp.where(kind, d_focal, 2.0 * positive * d_smooth) * scale
        head_sum[...] += d_heads
        high = d_heads.astype(BF16)
        rest_one = d_heads - high.astype(F32)
        mid = rest_one.astype(BF16)
        tiny = (rest_one - mid.astype(F32)).astype(BF16)
        three = jnp.concatenate([high, mid, tiny], axis=0)
        grad_head_ref[...] += jnp.dot(three, act, preferred_element_type=F32)
        d_act = lax.dot_general(
            three, head_three, (((0,), (0,)), ((), ())), preferred_element_type=F32
        )
        d_pre = jnp.where(pre > 0.0, d_act, 0.0).astype(BF16)
        d_ref[at_row(r, columns), :] = d_pre

        @pl.when(r == 0)
        def _():
            first_ref[...] = d_pre

        @pl.when(r == d_ref.shape[0] // columns - 1)
        def _():
            last_ref[...] = d_pre

        sums_ref[0:8, :] += jnp.sum(d_pre.astype(F32).reshape(columns // 8, 8, LANES), axis=0)
        return carry

    lax.fori_loop(0, d_ref.shape[0] // columns, row, 0)
    sums_ref[8:24, :] = jnp.broadcast_to(
        jnp.sum(head_sum[...], axis=1, keepdims=True), (outs, LANES)
    )
    sums_ref[24:32, :] = jnp.broadcast_to(
        jnp.sum(jnp.sum(loss_sum[...], axis=1, keepdims=True), axis=0, keepdims=True), (8, LANES)
    )


def region_forward(scale, bev, weights, bias, head, head_bias, labels, targets, columns):
    rows = labels.shape[0]
    outs = head.shape[0]
    return pl.pallas_call(
        functools.partial(region_kernel, columns),
        out_shape=(
            jax.ShapeDtypeStruct((rows * columns, LANES), BF16),
            jax.ShapeDtypeStruct((columns, LANES), BF16),
            jax.ShapeDtypeStruct((columns, LANES), BF16),
            jax.ShapeDtypeStruct((3 * outs, LANES), F32),
            jax.ShapeDtypeStruct((32, LANES), F32),
        ),
        in_specs=smem(1) + vmem(7),
        out_specs=vmem(5),
        scratch_shapes=[pltpu.VMEM((outs, columns), F32), pltpu.VMEM((outs, columns), F32)],
        compiler_params=params(),
        cost_estimate=work(16),
        name="region_forward",
    )(
        scale.reshape(1, 1),
        bev,
        weights,
        jnp.broadcast_to(bias.reshape(1, -1), (8, LANES)),
        head,
        jnp.broadcast_to(head_bias.reshape(-1, 1), (outs, LANES)),
        labels,
        targets,
    )


def region_order(w_all):
    three, _, channels, outs = w_all.shape
    depth_out = DEPTH // 2
    turned = w_all.reshape(three, three, channels // depth_out, depth_out, outs)
    turned = turned.transpose(0, 1, 3, 2, 4).reshape(three, three, channels, outs)
    return jnp.pad(turned, ((0, 0), (0, 0), (0, PAIRS * LANES - channels), (0, 0)))


def region_data_kernel(
    columns, edge_ref, d_ref, above_ref, below_ref, bev_ref, weight_ref,
    out_ref, first_ref, last_ref, sums_ref, taps_ref,
):
    rows = out_ref.shape[0] // columns
    width = PAIRS * LANES
    sums_ref[...] = jnp.zeros_like(sums_ref)

    def build(r, own):
        taps_ref[at_row(r, columns), 0:LANES] = from_right(own).astype(BF16)
        taps_ref[at_row(r, columns), LANES : 2 * LANES] = own.astype(BF16)
        taps_ref[at_row(r, columns), 2 * LANES :] = from_left(own).astype(BF16)

    def build_own(r, carry):
        build(r + 1, d_ref[at_row(r, columns), :].astype(F32))
        return carry

    build(0, jnp.where(edge_ref[0] > 0, above_ref[...].astype(F32), 0.0))
    lax.fori_loop(0, rows, build_own, 0)
    build(rows + 1, jnp.where(edge_ref[1] > 0, below_ref[...].astype(F32), 0.0))

    def row(r, carry):
        left = jnp.concatenate([taps_ref[at_row(r + 2 - b, columns), :] for b in range(3)], axis=1)
        total = jnp.dot(left, weight_ref[...], preferred_element_type=F32)
        alive = bev_ref[at_row(r + 1, columns), :].astype(F32) > 0.0
        kept = jnp.where(alive, total, 0.0).astype(BF16)
        out_ref[at_row(r, columns), :] = kept

        @pl.when(r == 0)
        def _():
            first_ref[...] = kept

        @pl.when(r == rows - 1)
        def _():
            last_ref[...] = kept

        sums_ref[...] += jnp.sum(kept.astype(F32).reshape(columns // 8, 8, width), axis=0)
        return carry

    lax.fori_loop(0, rows, row, 0)


def region_data(edges, d_rows, above, below, bev, weights, columns):
    width = PAIRS * LANES
    return pl.pallas_call(
        functools.partial(region_data_kernel, columns),
        out_shape=(
            jax.ShapeDtypeStruct((d_rows.shape[0], width), BF16),
            jax.ShapeDtypeStruct((columns, width), BF16),
            jax.ShapeDtypeStruct((columns, width), BF16),
            jax.ShapeDtypeStruct((8, width), F32),
        ),
        in_specs=smem(1) + vmem(5),
        out_specs=vmem(4),
        scratch_shapes=[pltpu.VMEM((d_rows.shape[0] + 2 * columns, 3 * LANES), BF16)],
        compiler_params=params(),
        cost_estimate=work(13),
        name="region_data",
    )(edges, d_rows, above, below, bev, weights)


def region_weight_kernel(columns, blocks, d_ref, bev_ref, out_ref, total, taps_ref):
    rows = d_ref.shape[0] // columns
    width = PAIRS * LANES
    depth_out = DEPTH // 2
    half = LANES // 2
    total[...] = jnp.zeros_like(total)

    def two(i, carry):
        for k in range(2):
            own = d_ref[at_row(i * 2 + k, columns), :].astype(F32)
            place = slice(k * columns, (k + 1) * columns)
            taps_ref[place, 0:LANES] = from_right(own).astype(BF16)
            taps_ref[place, LANES : 2 * LANES] = own.astype(BF16)
            taps_ref[place, 2 * LANES :] = from_left(own).astype(BF16)
        cells = jnp.concatenate(
            [
                bev_ref[pl.ds(pl.multiple_of((i * 2 + b) * columns, 32), 2 * columns), :]
                for b in range(3)
            ],
            axis=1,
        )
        total[...] += lax.dot_general(
            taps_ref[...], cells, (((0,), (0,)), ((), ())), preferred_element_type=F32
        )
        return carry

    lax.fori_loop(0, rows // 2, two, 0)
    share = half // blocks
    used = 9 * depth_out * half
    out_ref[used:, :] = jnp.zeros((out_ref.shape[0] - used, LANES), F32)
    for b in range(3):
        for e in range(3):
            for j in range(PAIRS):
                start = b * width + j * LANES
                turned = total[e * LANES : (e + 1) * LANES, start : start + LANES].T
                for k in range(min(2, depth_out - 2 * j)):
                    for q in range(blocks):
                        begin = k * half + q * share
                        base = ((q * 3 + b) * 3 + e) * share * depth_out
                        out_ref[pl.ds(base + 2 * j + k, share, stride=depth_out), :] = turned[
                            begin : begin + share, :
                        ]


def region_weight(d_own, bev, columns, blocks, total_rows):
    width = PAIRS * LANES
    return pl.pallas_call(
        functools.partial(region_weight_kernel, columns, blocks),
        out_shape=jax.ShapeDtypeStruct((total_rows, LANES), F32),
        in_specs=vmem(2),
        out_specs=vmem(1)[0],
        scratch_shapes=[
            pltpu.VMEM((3 * LANES, 3 * width), F32),
            pltpu.VMEM((2 * columns, 3 * LANES), BF16),
        ],
        compiler_params=params(),
        cost_estimate=work(10),
        name="region_weight",
    )(d_own, bev)


def prepare_kernel(
    slots, anc_count, device_rows, edge_ref, points_ref, count_ref, coord_ref, labels_ref,
    stats_ref, place_ref,
):
    voxels, width = points_ref.shape
    real = points_ref.shape[1] - 1
    features = 7
    lane = lax.broadcasted_iota(jnp.int32, (CHUNK, width), 1)
    ones_lane = features * slots
    total = jnp.zeros((width, width), F32)
    for i in range(voxels // CHUNK):
        block = points_ref[i * CHUNK : (i + 1) * CHUNK, :].astype(F32)
        valid = (lane % slots < count_ref[i * CHUNK : (i + 1) * CHUNK, :]) | (lane == ones_lane)
        block = jnp.where(valid, block, 0.0).astype(BF16)
        total = total + lax.dot_general(
            block, block, (((0,), (0,)), ((), ())), preferred_element_type=F32
        )
    row_at = lax.broadcasted_iota(jnp.int32, (width, width), 0)
    col_at = lax.broadcasted_iota(jnp.int32, (width, width), 1)
    same = (row_at % slots == col_at % slots) | (row_at == ones_lane)
    total = jnp.where(same & (row_at <= ones_lane) & (col_at < ones_lane), total, 0.0)
    rows = [
        jnp.sum(jnp.where(row_at // slots == k, total, 0.0), axis=0, keepdims=True)
        for k in range(features + 1)
    ]
    stacked = jnp.concatenate(rows, axis=0)
    col_eight = lax.broadcasted_iota(jnp.int32, (8, width), 1)
    lane_eight = lax.broadcasted_iota(jnp.int32, (8, LANES), 1)
    row_eight = lax.broadcasted_iota(jnp.int32, (8, LANES), 0)
    stats = jnp.zeros((8, LANES), F32)
    for k in range(features):
        picked = jnp.sum(jnp.where(col_eight // slots == k, stacked, 0.0), axis=1, keepdims=True)
        stats = stats + jnp.where(lane_eight == k, picked, 0.0)
    counted = jnp.sum(count_ref[...].astype(F32), axis=0, keepdims=True)
    found = jnp.zeros((1, 1), F32)
    for r in range(labels_ref.shape[0]):
        hits = jnp.where(labels_ref[r] == 1, 1.0, 0.0)
        found = found + jnp.sum(jnp.sum(hits, axis=1, keepdims=True), axis=0, keepdims=True)
    row = coord_ref[1:2, :]
    exists = coord_ref[3:4, :] > 0
    lists = []
    for q in range(anc_count):
        begin = q * device_rows - HALO
        lists.append(exists & (row >= begin) & (row < begin + device_rows + 2 * HALO))
    lists.append(exists & (row < HALO) & (edge_ref[0] > 0))
    lists.append(exists & (row >= anc_count * device_rows - HALO) & (edge_ref[1] > 0))
    lists += [exists & (row < 0)] * (8 - len(lists))
    member = jnp.concatenate([jnp.where(x, 1.0, 0.0) for x in lists], axis=0)
    before = (
        lax.broadcasted_iota(jnp.int32, (LANES, LANES), 0)
        < lax.broadcasted_iota(jnp.int32, (LANES, LANES), 1)
    )
    before = jnp.where(before, 1.0, 0.0).astype(BF16)
    carry = jnp.zeros((8, 1), F32)
    for i in range(voxels // LANES):
        part = member[:, i * LANES : (i + 1) * LANES]
        ahead = jnp.dot(part.astype(BF16), before, preferred_element_type=F32) + carry
        place_ref[:, i * LANES : (i + 1) * LANES] = jnp.where(part > 0.0, ahead, -1.0).astype(
            jnp.int32
        )
        carry = carry + jnp.sum(part, axis=1, keepdims=True)
    is_edge = lax.broadcasted_iota(jnp.int32, (8, 1), 0) >= anc_count
    need = carry / jnp.where(is_edge, float(EDGE_CAP), float(CAP))
    need = jnp.max(need, axis=0, keepdims=True)
    for k, value in enumerate((counted, found, need)):
        stats = stats + jnp.where((lane_eight == 8) & (row_eight == k), value, 0.0)
    stats_ref[...] = stats


def prepare(edges, points, counts, coords, labels, anc_count, device_rows, slots):
    voxels = points.shape[0]
    return pl.pallas_call(
        functools.partial(prepare_kernel, slots, anc_count, device_rows),
        out_shape=(
            jax.ShapeDtypeStruct((8, LANES), F32),
            jax.ShapeDtypeStruct((8, voxels), jnp.int32),
        ),
        in_specs=smem(1) + vmem(4),
        out_specs=vmem(2),
        compiler_params=params(),
        cost_estimate=work(4),
        name="prepare",
    )(edges, points, counts, coords, labels)


def exact_dot(left, right):
    return jnp.dot(left, right, preferred_element_type=F32, precision=lax.Precision.HIGHEST)


def batch_norm(stats, kernel, gain, shift):
    lanes = kernel.shape[1]
    moments = stats[:, 0:8]
    count = stats[0:1, 8:9]
    mixed = jnp.zeros((8, lanes), F32)
    for k in range(7):
        mixed = mixed + moments[:, k : k + 1] * kernel[k : k + 1, :]
    mean = mixed[7:8, :] / count
    second = jnp.sum(mixed * kernel, axis=0, keepdims=True) / count
    inv_std = lax.rsqrt(second - mean * mean + BN_EPSILON)
    return mixed, mean, inv_std, count


def first_layer(points, first_ref, scale, offset, valid):
    hidden = jnp.dot(points, first_ref[...], preferred_element_type=F32)
    act = jnp.where(valid, jnp.maximum(hidden * scale + offset, 0.0), 0.0)
    return act


def group_fold(values, combine):
    groups = values.shape[1] // LANES
    out = values[:, :LANES]
    for g in range(1, groups):
        out = combine(out, values[:, g * LANES : (g + 1) * LANES])
    out = combine(out, pltpu.roll(out, 32, 1))
    return combine(out, pltpu.roll(out, 64, 1))


def second_tail(pooled):
    lane = lax.broadcasted_iota(jnp.int32, pooled.shape, 1)
    return jnp.where(lane < 32, pooled, jnp.where(lane == 32, 1.0, 0.0)).astype(BF16)


def encode_kernel(
    slots, points_ref, count_ref, stats_ref, kernel_ref, gain_ref, first_ref, second_ref,
    feat_ref, share_ref, held,
):
    lanes = first_ref.shape[1]
    _, mean, inv_std, _ = batch_norm(stats_ref[...], kernel_ref[...], None, None)
    scale = gain_ref[0:1, :] * inv_std
    offset = gain_ref[1:2, :] - mean * scale
    count = count_ref[...]
    slot = lax.broadcasted_iota(jnp.int32, (CHUNK, lanes), 1) // 32
    act = first_layer(points_ref[...], first_ref, scale, offset, slot < count)
    tail = second_tail(group_fold(act, jnp.maximum))
    low = act.astype(BF16)
    top = jnp.full((CHUNK, LANES), -jnp.inf, F32)
    for g in range(lanes // LANES):
        left = jnp.concatenate([low[:, g * LANES : (g + 1) * LANES], tail], axis=1)
        part = jnp.dot(left, second_ref[...], preferred_element_type=F32)
        for s in range(min(4, slots - 4 * g)):
            p = 4 * g + s
            one = jnp.where(p < count, part[:, s * LANES : (s + 1) * LANES], -jnp.inf)
            held[p] = one
            top = jnp.maximum(top, one)
    ties = jnp.zeros((CHUNK, LANES), F32)
    for p in range(slots):
        ties = ties + jnp.where(held[p] == top, 1.0, 0.0)
    feat_ref[...] = jnp.maximum(top, 0.0)
    share_ref[...] = jnp.where(top > 0.0, 1.0 / ties, 0.0)


def encode(points, counts, stats, kernel, gain, first, second, slots):
    voxels, width = points.shape
    lanes = first.shape[1]
    whole = lambda *shape: pl.BlockSpec(shape, lambda i: (0,) * len(shape))
    block = lambda size: pl.BlockSpec((CHUNK, size), lambda i: (i, 0))
    return pl.pallas_call(
        functools.partial(encode_kernel, slots),
        grid=(voxels // CHUNK,),
        out_shape=(
            jax.ShapeDtypeStruct((voxels, LANES), F32),
            jax.ShapeDtypeStruct((voxels, LANES), F32),
        ),
        in_specs=[
            block(width),
            block(1),
            whole(8, LANES),
            whole(8, lanes),
            whole(8, lanes),
            whole(width, lanes),
            whole(2 * LANES, 4 * LANES),
        ],
        out_specs=[block(LANES), block(LANES)],
        scratch_shapes=[pltpu.VMEM((slots, CHUNK, LANES), F32)],
        compiler_params=params("arbitrary"),
        cost_estimate=work(19),
        name="encode",
    )(points, counts, stats, kernel, gain, first, second)


def decode_kernel(
    slots, points_ref, count_ref, stats_ref, kernel_ref, gain_ref, first_ref, second_ref,
    feat_ref, share_ref, d_feat_ref, first_out_ref, second_out_ref,
    first_sum, second_sum, joined,
):
    lanes = first_ref.shape[1]
    width = points_ref.shape[1]
    step = pl.program_id(0)

    @pl.when(step == 0)
    def _():
        first_sum[...] = jnp.zeros_like(first_sum)
        second_sum[...] = jnp.zeros_like(second_sum)

    _, mean, inv_std, _ = batch_norm(stats_ref[...], kernel_ref[...], None, None)
    scale = gain_ref[0:1, :] * inv_std
    offset = gain_ref[1:2, :] - mean * scale
    count = count_ref[...]
    points = points_ref[...]
    slot = lax.broadcasted_iota(jnp.int32, (CHUNK, lanes), 1) // 32
    act = first_layer(points, first_ref, scale, offset, slot < count)
    pooled = group_fold(act, jnp.maximum)
    tail = second_tail(pooled)
    low = act.astype(BF16)
    top = feat_ref[...]
    d_feat = d_feat_ref[...] * share_ref[...]
    d_tail = jnp.zeros((CHUNK, LANES), F32)
    for g in range(lanes // LANES):
        left = jnp.concatenate([low[:, g * LANES : (g + 1) * LANES], tail], axis=1)
        part = jnp.dot(left, second_ref[...], preferred_element_type=F32)
        pieces = []
        for s in range(4):
            p = 4 * g + s
            if p < slots:
                hit = (part[:, s * LANES : (s + 1) * LANES] == top) & (p < count)
                pieces.append(jnp.where(hit, d_feat, 0.0).astype(BF16))
            else:
                pieces.append(jnp.zeros((CHUNK, LANES), BF16))
        d_part = jnp.concatenate(pieces, axis=1)
        second_sum[...] += lax.dot_general(
            left, d_part, (((0,), (0,)), ((), ())), preferred_element_type=F32
        )
        d_left = lax.dot_general(
            d_part, second_ref[...], (((1,), (1,)), ((), ())), preferred_element_type=F32
        )
        joined[:, g * LANES : (g + 1) * LANES] = d_left[:, :LANES]
        d_tail = d_tail + d_left[:, LANES:]
    ties = group_fold(
        jnp.where(act == jnp.concatenate([pooled] * (lanes // LANES), axis=1), 1.0, 0.0), jnp.add
    )
    lane = lax.broadcasted_iota(jnp.int32, (CHUNK, LANES), 1)
    spread = jnp.where(lane < 32, d_tail, 0.0)
    spread = spread + pltpu.roll(spread, 32, 1)
    spread = (spread + pltpu.roll(spread, 64, 1)) / ties
    spread = jnp.concatenate([spread] * (lanes // LANES), axis=1)
    wide = jnp.concatenate([pooled] * (lanes // LANES), axis=1)
    d_act = joined[...] + jnp.where(act == wide, spread, 0.0)
    d_act = jnp.where(act > 0.0, d_act, 0.0)
    high = d_act.astype(BF16)
    rest = (d_act - high.astype(F32)).astype(BF16)
    for piece in (high, rest):
        first_sum[...] += lax.dot_general(
            points, piece, (((0,), (0,)), ((), ())), preferred_element_type=F32
        )

    @pl.when(step == pl.num_programs(0) - 1)
    def _():
        row_at = lax.broadcasted_iota(jnp.int32, (width, lanes), 0)
        col_at = lax.broadcasted_iota(jnp.int32, (width, lanes), 1)
        same = (row_at % slots == col_at // 32) | (row_at == 7 * slots)
        total = jnp.where(same & (col_at // 32 < slots), first_sum[...], 0.0)
        rows = [
            jnp.sum(jnp.where(row_at // slots == k, total, 0.0), axis=0, keepdims=True)
            for k in range(8)
        ]
        first_out_ref[...] = group_fold(jnp.concatenate(rows, axis=0), jnp.add)
        for s in range(4):
            cols = slice(s * LANES, (s + 1) * LANES)
            upper = second_sum[s * 32 : (s + 1) * 32, cols]
            lower = second_sum[LANES : LANES + 40, cols]
            if s == 0:
                second_out_ref[0:32, :] = upper
                second_out_ref[32:72, :] = lower
            else:
                second_out_ref[0:32, :] += upper
                second_out_ref[32:72, :] += lower


def decode(points, counts, stats, kernel, gain, first, second, feat, share, d_feat, slots):
    voxels, width = points.shape
    lanes = first.shape[1]
    whole = lambda *shape: pl.BlockSpec(shape, lambda i: (0,) * len(shape))
    block = lambda size: pl.BlockSpec((CHUNK, size), lambda i: (i, 0))
    return pl.pallas_call(
        functools.partial(decode_kernel, slots),
        grid=(voxels // CHUNK,),
        out_shape=(
            jax.ShapeDtypeStruct((8, LANES), F32),
            jax.ShapeDtypeStruct((72, LANES), F32),
        ),
        in_specs=[
            block(width),
            block(1),
            whole(8, LANES),
            whole(8, lanes),
            whole(8, lanes),
            whole(width, lanes),
            whole(2 * LANES, 4 * LANES),
            block(LANES),
            block(LANES),
            block(LANES),
        ],
        out_specs=[whole(8, LANES), whole(72, LANES)],
        scratch_shapes=[
            pltpu.VMEM((width, lanes), F32),
            pltpu.VMEM((2 * LANES, 4 * LANES), F32),
            pltpu.VMEM((CHUNK, lanes), F32),
        ],
        compiler_params=params("arbitrary"),
        cost_estimate=work(35),
        name="decode",
    )(points, counts, stats, kernel, gain, first, second, feat, share, d_feat)


def encoder_weights(w_one, w_two, bias_two, gain, shift, slots):
    features, c_one = w_one.shape
    groups = -(-slots // 4)
    lanes = groups * LANES
    width = -(-(features * slots + 1) // LANES) * LANES
    row_at = lax.broadcasted_iota(jnp.int32, (width, lanes), 0)
    col_at = lax.broadcasted_iota(jnp.int32, (width, lanes), 1)
    tall = jnp.pad(
        jnp.repeat(w_one, slots, axis=0), ((0, width - features * slots), (0, 0))
    )
    same = (row_at % slots == col_at // c_one) & (row_at < features * slots)
    first = jnp.where(same, jnp.tile(tall, (1, lanes // c_one)), jnp.zeros((), BF16))
    c_two = w_two.shape[1]
    row_two = lax.broadcasted_iota(jnp.int32, (LANES, 4 * c_two), 0)
    col_two = lax.broadcasted_iota(jnp.int32, (LANES, 4 * c_two), 1)
    upper = jnp.where(
        row_two // c_one == col_two // c_two, jnp.tile(w_two[:c_one], (4, 4)), jnp.zeros((), BF16)
    )
    lower = jnp.concatenate([w_two[c_one:], bias_two.reshape(1, -1)], axis=0)
    lower = jnp.pad(lower, ((0, LANES - lower.shape[0]), (0, 0)))
    second = jnp.concatenate([upper, jnp.tile(lower, (1, 4))], axis=0)
    kernel = jnp.pad(w_one.astype(F32), ((0, 1), (0, 0)))
    kernel = jnp.tile(kernel, (1, lanes // c_one))
    rows = jnp.pad(jnp.stack([gain, shift]).astype(F32), ((0, 6), (0, 0)))
    return first, second, kernel, jnp.tile(rows, (1, lanes // c_one))


def gather_lists_kernel(anc_count, offset_ref, feat_ref, digit_ref, place_ref, main_ref, up_ref, down_ref):
    source = jnp.concatenate([feat_ref[...].astype(BF16), digit_ref[...]], axis=1)
    voxels = source.shape[0]

    def pick(line, capacity, offset):
        want = place_ref[line : line + 1, :] - offset
        row_at = lax.broadcasted_iota(jnp.int32, (capacity, voxels), 0)
        chosen = jnp.where(want == row_at, 1.0, 0.0).astype(BF16)
        found = jnp.dot(chosen, source, preferred_element_type=F32)
        return found[:, :LANES].astype(BF16), found[:, LANES:].T

    for q in range(anc_count):
        rows, digits = pick(q, CAP, offset_ref[0])
        main_ref[q, 0:CAP, :] = rows
        lines = [
            digits[k : k + 1, i * LANES : (i + 1) * LANES]
            for k in range(3)
            for i in range(CAP // LANES)
        ]
        lines.append(jnp.zeros((32 - len(lines), LANES), F32))
        main_ref[q, CAP : CAP + 32, :] = jnp.concatenate(lines, axis=0).astype(BF16)
        main_ref[q, CAP + 32 :, :] = jnp.zeros((EDGE_CAP + 16, LANES), BF16)
    for side, edge_ref in enumerate((up_ref, down_ref)):
        rows, digits = pick(anc_count + side, EDGE_CAP, offset_ref[1])
        edge_ref[0:EDGE_CAP, :] = rows
        digits = jnp.concatenate([digits[0:8, :], jnp.zeros((8, LANES), F32)], axis=0)
        edge_ref[EDGE_CAP : EDGE_CAP + 16, :] = digits.astype(BF16)


def gather_lists(offsets, feat, digits, place, anc_count):
    return pl.pallas_call(
        functools.partial(gather_lists_kernel, anc_count),
        out_shape=(
            jax.ShapeDtypeStruct((anc_count, CAP + EDGE_CAP + 48, LANES), BF16),
            jax.ShapeDtypeStruct((EDGE_CAP + 16, LANES), BF16),
            jax.ShapeDtypeStruct((EDGE_CAP + 16, LANES), BF16),
        ),
        in_specs=smem(1) + vmem(3),
        out_specs=vmem(3),
        compiler_params=params(),
        cost_estimate=work(5),
        name="gather_lists",
    )(offsets, feat, digits, place)


def spread_lists_kernel(received_ref, where_ref, out_ref):
    total = received_ref.shape[0]
    lane = lax.broadcasted_iota(jnp.int32, (CHUNK, total), 1)
    chosen = jnp.where(where_ref[...] == lane, 1.0, 0.0).astype(BF16)
    out_ref[...] = jnp.dot(chosen, received_ref[...], preferred_element_type=F32)


def spread_lists(received, where):
    voxels = where.shape[0]
    total = received.shape[0]
    return pl.pallas_call(
        spread_lists_kernel,
        grid=(voxels // CHUNK,),
        out_shape=jax.ShapeDtypeStruct((voxels, LANES), F32),
        in_specs=[
            pl.BlockSpec((total, LANES), lambda i: (0, 0)),
            pl.BlockSpec((CHUNK, 1), lambda i: (i, 0)),
        ],
        out_specs=pl.BlockSpec((CHUNK, LANES), lambda i: (i, 0)),
        compiler_params=params("arbitrary"),
        cost_estimate=work(6),
        name="spread_lists",
    )(received, where)


def finish_kernel(stats_ref, kernel_ref, gain_ref, sums_ref, out_ref):
    kernel = kernel_ref[:, :LANES]
    mixed, mean, inv_std, count = batch_norm(stats_ref[...], kernel, None, None)
    sums = sums_ref[...]
    total_shift = sums[7:8, :]
    total_gain = inv_std * (jnp.sum(kernel * sums, axis=0, keepdims=True) - mean * total_shift)
    slope = gain_ref[0:1, :LANES] * inv_std
    for k in range(7):
        first = stats_ref[7:8, k : k + 1]
        pull = total_shift * first + total_gain * inv_std * (mixed[k : k + 1, :] - mean * first)
        out_ref[k : k + 1, :] = slope * (sums[k : k + 1, :] - pull / count)
    out_ref[7:8, :] = total_gain
    out_ref[8:16, :] = jnp.broadcast_to(total_shift, (8, LANES))


def finish_encoder(stats, kernel, gain, sums):
    return pl.pallas_call(
        finish_kernel,
        out_shape=jax.ShapeDtypeStruct((16, LANES), F32),
        in_specs=vmem(4),
        out_specs=vmem(1)[0],
        compiler_params=params(),
        cost_estimate=work(1),
        name="finish_encoder",
    )(stats, kernel, gain, sums)


def everyone(values, axes):
    count = 1
    for axis in axes:
        count *= lax.axis_size(axis)
    copies = jnp.broadcast_to(values[None], (count,) + values.shape)
    return lax.all_to_all(copies, axes, 0, 0)


def neighbour_rows(first, last):
    axes = ("tile", "anc")
    count = lax.axis_size("tile") * lax.axis_size("anc")
    down = [(i, i + 1) for i in range(count - 1)]
    return lax.ppermute(last, axes, down), lax.ppermute(first, axes, [(j, i) for i, j in down])


def sum_chunk(rows, axes):
    devices = 1
    for axis in axes:
        devices *= lax.axis_size(axis)
    parts = rows.reshape(devices, -1, rows.shape[1])
    return jnp.sum(lax.all_to_all(parts, axes, 0, 0), axis=0)


def shard_windows(segments, shard, count):
    windows = []
    for a in range(count):
        begin, end = a * shard, (a + 1) * shard
        at = 0
        pieces = []
        for name, size in segments:
            low, high = max(begin, at), min(end, at + size)
            if low < high:
                pieces.append((name, low - at, high - at))
            at += size
        windows.append(pieces)
    return windows


def on_device(
    points,
    npoints,
    coords,
    labels,
    targets,
    w_vfe1,
    w_vfe2,
    w_mid,
    w_rpn,
    w_head,
    bn_gain,
    biases,
    master,
    moment1,
    moment2,
):
    both = ("tile", "anc")
    anc_count = lax.axis_size("anc")
    tile_count = lax.axis_size("tile")
    anc = lax.axis_index("anc")
    tile = lax.axis_index("tile")
    device_rows = labels.shape[1]
    columns = labels.shape[2]
    blocks = device_rows // BLOCK_ROWS
    tile_rows = device_rows * anc_count
    all_rows = tile_rows * tile_count
    slots = points.shape[1]
    voxels = points.shape[2]
    c_vfe = w_vfe1.shape[1]
    c_vox = w_vfe2.shape[1]
    c_mid = w_mid.shape[4]
    c_rpn = w_rpn.shape[3]
    outs = w_head.shape[1]
    shift = biases[:c_vfe]
    bias_two = biases[c_vfe : c_vfe + c_vox]
    bias_mid, bias_rpn, bias_head = jnp.split(
        biases[c_vfe + c_vox :].astype(F32), [c_mid, c_mid + c_rpn]
    )

    def joined(row):
        return (row % CROP_ROWS != CROP_ROWS // 2) & (row > 0) & (row < all_rows)

    padded = -(-voxels // CHUNK) * CHUNK
    width = -(-(points.shape[0] * slots + 1) // LANES) * LANES
    flat_points = points.reshape(-1, voxels).T
    flat_points = jnp.pad(
        flat_points, ((0, padded - voxels), (0, width - flat_points.shape[1]))
    )
    lane = lax.broadcasted_iota(jnp.int32, flat_points.shape, 1)
    flat_points = jnp.where(lane == points.shape[0] * slots, jnp.ones((), BF16), flat_points)
    counts = jnp.pad(npoints, (0, padded - voxels)).reshape(padded, 1)
    layer = jnp.pad(coords[:, 0], (0, padded - voxels))
    row = jnp.pad(coords[:, 1] - tile * tile_rows, (0, padded - voxels))
    column = jnp.pad(coords[:, 2], (0, padded - voxels))
    exists = (jnp.arange(padded) < voxels).astype(jnp.int32)
    lines = jnp.pad(jnp.stack([layer, row, column, exists]), ((0, 4), (0, 0)))
    tile_edges = jnp.stack([joined(tile * tile_rows), joined((tile + 1) * tile_rows)])
    stats, place = prepare(
        tile_edges.astype(jnp.int32),
        flat_points,
        counts,
        lines,
        labels.transpose(1, 0, 2),
        anc_count,
        device_rows,
        slots,
    )
    sent, w_mid, w_rpn = lax.optimization_barrier((stats, w_mid, w_rpn))
    gathered = everyone(sent, both)
    weights = middle_weights(w_mid)
    data_weights = middle_data_weights(w_mid)
    region = everyone(w_rpn, ("anc",)).transpose(1, 2, 0, 3, 4)
    region = region_order(region.reshape(w_rpn.shape[:2] + (-1, c_rpn)))
    stats = jnp.sum(gathered, axis=0)
    count_pos = stats[1, 8]
    rounds = jnp.ceil(jnp.max(gathered[:, 2, 8])).astype(jnp.int32)

    first, second, kernel, gain_rows = encoder_weights(
        w_vfe1, w_vfe2, bias_two, bn_gain, shift, slots
    )
    feat, share = encode(flat_points, counts, stats, kernel, gain_rows, first, second, slots)

    digits = jnp.stack(
        [(layer + 1) * exists, column // 2 * exists, (row * 2 + column % 2) * exists], axis=1
    )
    digits = jnp.pad(digits, ((0, 0), (0, LANES - 3))).astype(BF16)
    slot_own = sum(
        jnp.where(row // device_rows == q, place[q], 0) for q in range(anc_count)
    )
    owner = jnp.clip(row // device_rows, 0, anc_count - 1)
    in_tile = lax.axis_size("tile")
    upward = [(i + 1, i) for i in range(in_tile - 1)]
    downward = [(i, i + 1) for i in range(in_tile - 1)]

    def exchange(number):
        offsets = jnp.stack([number * CAP, number * EDGE_CAP]).astype(jnp.int32)
        main, up, down = gather_lists(offsets, feat, digits, place, anc_count)
        from_below = lax.ppermute(up, "tile", upward)
        from_above = lax.ppermute(down, "tile", downward)
        main = lax.dynamic_update_slice(main, from_above[None], (0, CAP + 32, 0))
        main = lax.dynamic_update_slice(main, from_below[None], (anc_count - 1, CAP + 32, 0))
        got = lax.all_to_all(main, "anc", 0, 0)
        words = got[:, CAP : CAP + 32].reshape(anc_count, -1).astype(jnp.int32)
        start = CAP + 32 + EDGE_CAP
        edge_words = got[:, start : start + 16].astype(jnp.int32)

        def word(k):
            gap = jnp.zeros((anc_count, 32), jnp.int32)
            parts = [words[:, k * CAP : (k + 1) * CAP], gap, edge_words[:, k], gap[:, :16]]
            return jnp.concatenate(parts, axis=1)

        high, half, mixed = word(0), word(1), word(2)
        local = mixed // 2 - anc * device_rows
        is_edge = lax.broadcasted_iota(jnp.int32, local.shape, 1) >= CAP
        local = local + jnp.where(is_edge, jnp.where(anc == 0, -tile_rows, tile_rows), 0)
        cross = half * 2 + mixed % 2
        scatter_at, own_at = [], []
        for k in range(blocks):
            line = local - k * BLOCK_ROWS
            tall = BLOCK_ROWS + 2 * HALO
            inside = (high > 0) & (line >= -HALO) & (line < BLOCK_ROWS + HALO)
            spot = ((high - 1) * tall + line + HALO) * columns + cross
            scatter_at.append(jnp.where(inside, spot, DEPTH * tall * columns).reshape(-1))
            inside = (high > 0) & (line >= 0) & (line < BLOCK_ROWS)
            spot = ((high - 1) * BLOCK_ROWS + line) * columns + cross
            spot = jnp.where(inside, spot, DEPTH * BLOCK_ROWS * columns)
            own_at.append(spot[:, :CAP].reshape(-1))
        return got.reshape(-1, LANES), scatter_at, own_at

    feats, scatter_at, own_at = exchange(0)
    grids = [scatter_rows(index, feats, None, columns) for index in scatter_at]

    def more(state):
        return state[0] < rounds

    def another(state):
        number, held = state
        rows, index, _ = exchange(number)
        held = [scatter_rows(at, rows, old, columns) for at, old in zip(index, held)]
        return number + 1, held

    _, grids = lax.while_loop(more, another, (jnp.int32(1), grids))

    first_row = tile * tile_rows + anc * device_rows
    bevs, edges = [], []
    for k in range(blocks):
        top = first_row + k * BLOCK_ROWS
        edges.append(jnp.stack([joined(top), joined(top + BLOCK_ROWS)]).astype(jnp.int32))
        bevs.append(middle_forward(edges[k], grids[k], weights, bias_mid, columns))

    lanes = region.shape[2]
    region_in = region.transpose(0, 2, 1, 3).reshape(3 * lanes, 3 * c_rpn)
    region_back = region.transpose(0, 1, 3, 2).reshape(9 * c_rpn, lanes)
    wide_labels = jnp.repeat(labels.transpose(1, 0, 2), outs // 2, axis=1)
    wide_targets = jnp.pad(targets.transpose(2, 0, 1, 3), ((0, 0), (0, 0), (1, 0), (0, 0)))
    wide_targets = wide_targets.reshape(device_rows, outs, columns)
    scale = 1.0 / count_pos
    d_rows, head_sums, row_sums = [], 0.0, 0.0
    d_first, d_last = [], []
    for k in range(blocks):
        here = slice(k * BLOCK_ROWS, (k + 1) * BLOCK_ROWS)
        d_block, top_row, end_row, heads, sums = region_forward(
            scale,
            bevs[k],
            region_in,
            bias_rpn,
            w_head.T,
            bias_head,
            wide_labels[here],
            wide_targets[here],
            columns,
        )
        d_rows.append(d_block)
        d_first.append(top_row)
        d_last.append(end_row)
        head_sums = head_sums + heads
        row_sums = row_sums + sums

    def beside(firsts, lasts):
        above, below = neighbour_rows(firsts[0], lasts[-1])
        return [above] + lasts[:-1], firsts[1:] + [below]

    devices = anc_count * tile_count
    unit = devices * 8
    above, below = beside(d_first, d_last)
    region_rows = -(-(9 * w_rpn.shape[2] * anc_count) // unit) * unit
    grad_region = sum(
        region_weight(d_rows[k], bevs[k], columns, anc_count, region_rows) for k in range(blocks)
    )
    d_rows, grad_region = lax.optimization_barrier((d_rows, grad_region))
    region_chunk = sum_chunk(grad_region, both)
    d_mids, mid_sums = [], 0.0
    mid_first, mid_last = [], []
    for k in range(blocks):
        d_block, top_row, end_row, sums = region_data(
            edges[k], d_rows[k], above[k], below[k], bevs[k], region_back, columns
        )
        d_mids.append(d_block)
        mid_first.append(top_row)
        mid_last.append(end_row)
        mid_sums = mid_sums + sums
    above, below = beside(mid_first, mid_last)
    middle_size = w_mid.size
    tail_size = c_rpn * outs + bn_gain.shape[0] + biases.shape[0]
    used = middle_size // LANES
    middle_rows = -(-max(used - (-tail_size // LANES), LARGE_ROWS) // unit) * unit
    grad_mid = sum(
        middle_weight(grids[k], d_mids[k], columns, middle_rows) for k in range(blocks)
    )

    head_three = head_sums.reshape(3, outs, c_rpn)
    grad_head = (head_three[0] + head_three[1] + head_three[2]).T
    grad_bias_mid = jnp.sum(mid_sums, axis=0)[: c_mid * DEPTH // 2].reshape(-1, c_mid).sum(axis=0)
    grad_bias_rpn = jnp.sum(row_sums[:8], axis=0)
    tail = jnp.concatenate(
        [
            grad_head.reshape(-1),
            jnp.zeros((c_vfe + c_vfe + c_vox,), F32),
            grad_bias_mid,
            grad_bias_rpn,
            row_sums[8 : 8 + outs, 0],
        ]
    )
    tail_rows = jnp.pad(tail, (0, -tail.shape[0] % LANES)).reshape(-1, LANES)
    grad_mid = lax.dynamic_update_slice(grad_mid, tail_rows, (used, 0))
    own_at, grad_mid, region_chunk = lax.optimization_barrier((own_at, grad_mid, region_chunk))
    middle_chunk = sum_chunk(grad_mid, both)
    region_full = lax.all_gather(region_chunk, both, axis=0, tiled=True)

    def collect(number, own_index, chunk):
        lists = sum(
            middle_data(
                own_index[k], edges[k], d_mids[k], above[k], below[k], data_weights, columns
            )
            for k in range(blocks)
        )
        lists, chunk = lax.optimization_barrier((lists, chunk))
        back = lax.all_to_all(lists.reshape(anc_count, CAP, LANES), "anc", 0, 0)
        mine = slot_own - number * CAP
        known = (exists > 0) & (mine >= 0) & (mine < CAP)
        where = jnp.where(known, owner * CAP + mine, -1).reshape(padded, 1)
        return spread_lists(back.reshape(-1, LANES), where), chunk

    d_feat, middle_chunk = collect(0, own_at, middle_chunk)
    middle_full = lax.all_gather(middle_chunk, both, axis=0, tiled=True)

    def collect_more(state):
        number, held = state
        _, _, index = exchange(number)
        return number + 1, held + collect(number, index, ())[0]

    _, d_feat = lax.while_loop(more, collect_more, (jnp.int32(1), d_feat))
    d_feat, region_full = lax.optimization_barrier((d_feat, region_full))
    first_sums, second_sums = decode(
        flat_points, counts, stats, kernel, gain_rows, first, second, feat, share, d_feat, slots
    )

    late = jnp.concatenate([first_sums, second_sums, row_sums[24:32]], axis=0)
    rows = late.shape[0]
    late = late.reshape(devices, -1)
    late = jnp.sum(lax.all_to_all(late[:, None], both, 0, 0), axis=0)
    late = everyone(late, both).reshape(rows, LANES)
    encoder = finish_encoder(stats, kernel, gain_rows, late[:8])
    second_total = late[8 : 8 + second_sums.shape[0]]
    loss = late[rows - 1, 0] / count_pos
    encoder_flat = jnp.concatenate(
        [encoder[:7, :c_vfe].reshape(-1), second_total[: 2 * c_vfe].reshape(-1)]
    )
    tail_late = jnp.concatenate(
        [
            jnp.zeros((c_rpn * outs,), F32),
            encoder[7, :c_vfe],
            encoder[8, :c_vfe],
            second_total[2 * c_vfe],
            jnp.zeros((c_mid + c_rpn + outs,), F32),
        ]
    )
    shard = master.shape[0]
    segments = (
        ("region", w_rpn.size * anc_count),
        ("encoder", encoder_flat.shape[0]),
        ("middle", middle_size),
        ("tail", tail_size),
    )
    region_flat = region_full.reshape(-1)
    middle_flat = middle_full.reshape(-1)

    def assemble(pieces):
        parts = []
        for name, low, high in pieces:
            if name == "encoder":
                parts.append(encoder_flat[low:high])
            elif name == "region":
                parts.append(region_flat[low:high])
            elif name == "middle":
                parts.append(middle_flat[low:high])
            else:
                early = middle_flat[middle_size + low : middle_size + high]
                parts.append(early + tail_late[low:high])
        return jnp.concatenate(parts) if len(parts) > 1 else parts[0]

    reduced = None
    for a, pieces in enumerate(shard_windows(segments, shard, anc_count)):
        one = assemble(pieces)
        reduced = one if a == 0 else jnp.where(anc == a, one, reduced)
    square_sum = jnp.sum(region_full * region_full) + jnp.sum(middle_full * middle_full)
    square_sum = square_sum + jnp.sum(encoder_flat * encoder_flat) + jnp.sum(tail_late * tail_late)
    norm_value = jnp.sqrt(square_sum)
    clipped = reduced * jnp.minimum(1.0, CLIP_LIMIT / (norm_value + 1e-06))
    first_new = BETA_FIRST * moment1 + (1.0 - BETA_FIRST) * clipped
    second_new = BETA_SECOND * moment2 + (1.0 - BETA_SECOND) * clipped * clipped
    first_hat = first_new / (1.0 - BETA_FIRST**STEP_NUMBER)
    second_hat = second_new / (1.0 - BETA_SECOND**STEP_NUMBER)
    updated = master - LEARN_RATE * (
        first_hat / (jnp.sqrt(second_hat) + ADAM_EPSILON) + WEIGHT_DECAY * master
    )
    return (updated, first_new, second_new, loss, norm_value)


def solution(mesh):
    placed = (
        P(None, None, ("tile", "anc")),
        P(("tile", "anc")),
        P(("tile", "anc"), None),
        P(None, ("tile", "anc"), None),
        P(None, None, ("tile", "anc"), None),
        P(),
        P(),
        P(),
        P(None, None, "anc", None),
        P(),
        P(),
        P(),
        P("anc"),
        P("anc"),
        P("anc"),
    )
    return jax.shard_map(
        on_device,
        mesh=mesh,
        in_specs=placed,
        out_specs=(P("anc"), P("anc"), P("anc"), P(), P()),
        check_vma=False,
    )
```

time: 1870 us -> 457 us (0.24)
  local copies, waits for them, and re-layouts: 741 us -> 52.3 us
  waiting for transfers between devices: 480 us -> 41.2 us
  matrix products: 305 us -> 0 us
  Pallas kernels: 0 us -> 205 us
  blocking collectives: 130 us -> 0 us
  other arithmetic: 151 us -> 27.3 us
  starting transfers between devices: 20.9 us -> 94 us
    reduce_scatter x2 -> x0, waiting for transfers between devices: 243 us -> none  [the longest x1 170 us: on_device(): lax.psum_scatter(middle_bev, 'anc', scatter_dimension=2, tiled=True)]
    unnamed x138 -> x79, local copies, waits for them, and re-layouts: 224 us -> 5.91 us
    conv_general_dilated x3 -> x0, matrix products: 206 us -> none  [the longest x1 182 us: on_device(): lax.conv_general_dilated(grid_rim[None], w_mid, (2, 1, 1), ((1, 0), (0, 0...]
    pallas_call x0 -> x13, Pallas kernels: none -> 205 us  [the longest x1 35.1 us: decode(): pl.pallas_call(functools.partial(decode_kernel, slots), grid=(voxels // C...]
    conv_general_dilated x14 -> x0, local copies, waits for them, and re-layouts: 175 us -> none  [the longest x4 134 us: on_device(): lax.conv_general_dilated(grid_rim[None], w_mid, (2, 1, 1), ((1, 0), (0, 0...]
    psum x4 -> x0, blocking collectives: 130 us -> none  [the longest x2 81.8 us: on_device(): lax.psum((jnp.sum(hidden_one * validity, axis=(1, 2)), jnp.sum(hidden_one...]
    gather x2 -> x0, local copies, waits for them, and re-layouts: 119 us -> none  [on_device(): picked = d_mid_table[gather_index] * usable[:, :, None].astype(jnp.bfloat16)]
    dot_general x19 -> x0, matrix products: 98.6 us -> none  [the longest x9 22.4 us: on_device(): jnp.einsum('rci,rco->io', bev_padded[row_off:row_off + tile_rows, col_off...]
  transfers between devices with their start and end apart: 14 -> 16, of which waited for: 12 -> 8; matrix products, arithmetic and copies ran while one was open for 4% -> 10% of each run, Pallas kernels for 0% -> 24%
where the time goes in v1:
time: 457 us; the launch traced here: 450 us
  Pallas kernels  205 us (45%)
  starting transfers between devices  94 us (21%)
  local copies, waits for them, and re-layouts  52.3 us (11%)
  waiting for transfers between devices  41.2 us (9%)
  other arithmetic  27.3 us (6%)
  between operations  22.8 us (5%)
  loops' own time  7.82 us (2%)
    all_to_all x2, starting transfers between devices, sum_chunk(): return jnp.sum(lax.all_to_all(parts, axes, 0, 0), axis=0)  36.4 us
    pallas_call x1, Pallas kernels, decode(): pl.pallas_call(functools.partial(decode_kernel, slots), grid=(voxels // C...  35.1 us
    pallas_call x1, Pallas kernels, middle_data(): pl.pallas_call(functools.partial(middle_data_kernel, count, columns), out...  27.1 us
    pallas_call x1, Pallas kernels, middle_forward(): pl.pallas_call(functools.partial(middle_kernel, columns), out_shape=jax.S...  26.4 us
    pallas_call x1, Pallas kernels, middle_weight(): pl.pallas_call(functools.partial(middle_weight_kernel, columns), out_shap...  25.3 us
    pallas_call x1, Pallas kernels, encode(): pl.pallas_call(functools.partial(encode_kernel, slots), grid=(voxels // C...  19.3 us
    all_to_all x1, starting transfers between devices, on_device(): late = jnp.sum(lax.all_to_all(late[:, None], both, 0, 0), axis=0)  18.7 us
    pallas_call x1, Pallas kernels, region_forward(): pl.pallas_call(functools.partial(region_kernel, columns), out_shape=(jax....  16.7 us
  transfers between devices with their start and end apart: 16, of which 8 were waited for; matrix products, arithmetic and copies ran while one was open for 10% of the time, Pallas kernels for 24%

profile of v1, /device:TPU:0, one launch (start us, length us, event | category | flops | bytes accessed | tf_op | source)
XLA Modules:
  0.0 450.2 jit_solution(11917693287148403895)
XLA Ops:
  17.9 3.5 prepare.1
  27.7 7.5 %all-to-all-start.3 = ((f32[32,8,128]{2,1,0:T(8,128)}), f32[32,8,128]{2,1,0:T(8,128)S(1)}, u32[]{:S(2)}, u32[]{:S(2)}) async-start(f32[32,8,128]{2,1,0:T(8,128)} %broadcast_in_dim.141), calls=%async_computation.3 | async-start | bytes 262144 | tf_op jit(solution)/shard_map/all_to_all | solution.py:1048
  37.9 5.5 %all-to-all-done.3 = f32[32,8,128]{2,1,0:T(8,128)S(1)} async-done(((f32[32,8,128]{2,1,0:T(8,128)}), f32[32,8,128]{2,1,0:T(8,128)S(1)}, u32[]{:S(2)}, u32[]{:S(2)}) %all-to-all-start.3) | async-done | bytes 131104 | tf_op jit(solution)/shard_map/all_to_all | solution.py:1048
  44.1 19.3 %encode.1 = (f32[1920,128]{1,0:T(8,128)S(1)}, f32[1920,128]{1,0:T(8,128)}) custom-call(bf16[1920,256]{1,0:T(8,128)(2,1)} %pad_select_fusion.points_ref, s32[1920,1]{1,0:T(8,128)} %reshape.334.count_ref, f32[8,128]{1,0:T(8,128)} %reduce_sum.99.stats_ref, f32[8,1152]{1,0:T(8,128)} %tile.27.kernel_ref, f32[8,1152]{1,0:T(8,128)} %tile.58.gain_ref, ...), custom_call_target="tpu_custom_call" | custom-call | flops 19 | bytes 57000000 | tf_op jit(solution)/shard_map/encode/pallas_call | solution.py:771
  63.9 5.2 %gather_lists.11 = (bf16[4,944,128]{2,1,0:T(8,128)(2,1)}, bf16[144,128]{1,0:T(8,128)(2,1)}, bf16[144,128]{1,0:T(8,128)(2,1)}) custom-call(s32[2]{0:T(128)} %broadcast_84_offset_ref.2.offset_ref, f32[1920,128]{1,0:T(8,128)S(1)} %get-tuple-element.846.feat_ref, bf16[1920,128]{1,0:T(8,128)(2,1)S(1)} %pad.73.digit_ref, s32[8,1920]{1,0:T(8,128)S(1)} %get-tuple-element.848.place_ref), custom_call_target="tpu_custom_call" | custom-call | flops 5 | bytes 15000000 | tf_op jit(solution)/shard_map/gather_lists/pallas_call | solution.py:976
  69.1 2.7 collective-permute-start.4
  72.8 3.5 all-to-all-start.5
  78.3 4.0 collective-permute-done.5
  82.9 4.5 %all-to-all-done.5 = bf16[4,3,3,80,128]{4,3,2,1,0:T(8,128)(2,1)S(1)} async-done(((bf16[4,3,3,80,128]{4,3,2,1,0:T(8,128)(2,1)}), bf16[4,3,3,80,128]{4,3,2,1,0:T(8,128)(2,1)S(1)}, u32[]{:S(2)}, u32[]{:S(2)}) %all-to-all-start.5) | async-done | bytes 737312 | tf_op jit(solution)/shard_map/all_to_all | solution.py:1048
  87.4 3.5 all-to-all-start.4
  95.7 2.3 pad_maximum_fusion.weight_ref
  110.8 15.3 %grid_scatter.6 = bf16[56320,128]{1,0:T(8,128)(2,1)} custom-call(s32[3776]{0:T(1024)} %fusion.36.refs_0_, bf16[3776,128]{1,0:T(8,128)(2,1)} %bitcast.182), custom_call_target="tpu_custom_call" | custom-call | flops 15 | bytes 45000000 | tf_op jit(solution)/shard_map/grid_scatter/pallas_call | solution.py:111
  127.4 26.4 %middle_forward.1.bev_ref = bf16[4928,384]{1,0:T(8,128)(2,1)} custom-call(s32[2]{0:T(128)S(1)} %add_convert_fusion.1.edge_ref, bf16[56320,128]{1,0:T(8,128)(2,1)} %get-tuple-element.419.grid_ref, bf16[2,1152,256]{2,1,0:T(8,128)(2,1)} %pad_maximum_fusion.weight_ref, f32[8,128]{1,0:T(8,128)} %tile.67.bias_ref), custom_call_target="tpu_custom_call" | custom-call | flops 26 | bytes 78000000 | tf_op jit(solution)/shard_map/middle_forward/pallas_call | solution.py:176
  155.0 16.7 %region_forward.1 = (bf16[4224,128]{1,0:T(8,128)(2,1)}, bf16[352,128]{1,0:T(8,128)(2,1)}, bf16[352,128]{1,0:T(8,128)(2,1)}, f32[48,128]{1,0:T(8,128)}, f32[32,128]{1,0:T(8,128)}) custom-call(f32[1,1]{1,0:T(1,128)S(6)} %div.124.scale_ref, bf16[4928,384]{1,0:T(8,128)(2,1)} %middle_forward.1.bev_ref, bf16[1152,384]{1,0:T(8,128)(2,1)} %bitcast.191, ...), custom_call_target="tpu_custom_call" | custom-call | flops 16 | bytes 48000000 | tf_op jit(solution)/shard_map/region_forward/pallas_call | solution.py:458
  171.7 10.3 %region_weight.1 = f32[3072,128]{1,0:T(8,128)} custom-call(bf16[4224,128]{1,0:T(8,128)(2,1)} %get-tuple-element.423.d_ref, bf16[4928,384]{1,0:T(8,128)(2,1)} %middle_forward.1.bev_ref), custom_call_target="tpu_custom_call" | custom-call | flops 10 | bytes 30000000 | tf_op jit(solution)/shard_map/region_weight/pallas_call | solution.py:600
  182.0 4.0 all-to-all-start.6
  195.6 12.7 %region_data.1 = (bf16[4224,384]{1,0:T(8,128)(2,1)S(1)}, bf16[352,384]{1,0:T(8,128)(2,1)}, bf16[352,384]{1,0:T(8,128)(2,1)}, f32[8,384]{1,0:T(8,128)}) custom-call(s32[2]{0:T(128)S(1)} %add_convert_fusion.1.edge_ref, bf16[4224,128]{1,0:T(8,128)(2,1)} %get-tuple-element.423.d_ref, bf16[352,128]{1,0:T(8,128)(2,1)} %copy-done.12, bf16[352,128]{1,0:T(8,128)(2,1)} %copy-done.13, ...), custom_call_target="tpu_custom_call" | custom-call | flops 13 | bytes 39000000 | tf_op jit(solution)/shard_map/region_data/pallas_call | solution.py:537
  208.3 25.3 %middle_weight.1 = f32[2304,128]{1,0:T(8,128)} custom-call(bf16[56320,128]{1,0:T(8,128)(2,1)} %get-tuple-element.419.grid_ref, bf16[4224,384]{1,0:T(8,128)(2,1)S(1)} %get-tuple-element.852.d_ref), custom_call_target="tpu_custom_call" | custom-call | flops 26 | bytes 78000000 | tf_op jit(solution)/shard_map/middle_weight/pallas_call | solution.py:348
  237.4 32.4 %all-to-all-start.7 = ((f32[32,72,128]{2,1,0:T(8,128)}), f32[32,72,128]{2,1,0:T(8,128)}, u32[]{:S(2)}, u32[]{:S(2)}) async-start(f32[32,72,128]{2,1,0:T(8,128)} %bitcast.179), calls=%async_computation.7 | async-start | bytes 2359296 | tf_op jit(solution)/shard_map/all_to_all | solution.py:1063
  279.5 2.5 collective-permute-done.9.below_ref
  282.8 27.1 %middle_data.6 = bf16[3072,128]{1,0:T(8,128)(2,1)} custom-call(s32[3072]{0:T(1024)} %reshape.302.index_ref, s32[2]{0:T(128)S(1)} %add_convert_fusion.1.edge_ref, bf16[4224,384]{1,0:T(8,128)(2,1)S(1)} %get-tuple-element.852.d_ref, bf16[352,384]{1,0:T(8,128)(2,1)S(1)} %collective-permute-done.8.above_ref, ...), custom_call_target="tpu_custom_call" | custom-call | flops 30 | bytes 90000000 | tf_op jit(solution)/shard_map/middle_data/pallas_call | solution.py:271
  311.8 10.6 %all-to-all-start.8 = ((bf16[4,768,128]{2,1,0:T(8,128)(2,1)}), bf16[4,768,128]{2,1,0:T(8,128)(2,1)}, u32[]{:S(2)}, u32[]{:S(2)}) async-start(bf16[4,768,128]{2,1,0:T(8,128)(2,1)} %bitcast.192), calls=%async_computation.8 | async-start | bytes 1572864 | tf_op jit(solution)/shard_map/all_to_all | solution.py:1319
  324.9 9.3 %all-to-all-done.8 = bf16[4,768,128]{2,1,0:T(8,128)(2,1)} async-done(((bf16[4,768,128]{2,1,0:T(8,128)(2,1)}), bf16[4,768,128]{2,1,0:T(8,128)(2,1)}, u32[]{:S(2)}, u32[]{:S(2)}) %all-to-all-start.8) | async-done | bytes 786464 | tf_op jit(solution)/shard_map/all_to_all | solution.py:1319
  334.2 6.4 %spread_lists.6 = f32[1920,128]{1,0:T(8,128)} custom-call(bf16[3072,128]{1,0:T(8,128)(2,1)} %bitcast.53.received_ref, s32[1920,1]{1,0:T(8,128)} %reshape.335.where_ref), custom_call_target="tpu_custom_call" | custom-call | flops 6 | bytes 18000000 | tf_op jit(solution)/shard_map/spread_lists/pallas_call | solution.py:1001
  340.6 7.6 %while.28 = (s32[]{:T(128)}, f32[1920,128]{1,0:T(8,128)}, s32[]{:T(128)}, f32[1920,128]{1,0:T(8,128)}, bf16[1920,128]{1,0:T(8,128)(2,1)}, /*index=5*/s32[8,1920]...) while((s32[]{:T(128)}, f32[1920,128]{1,0:T(8,128)}, ...), condition=%wide.region_10.11_spmd.clone, body=%wide.region_9.10_spmd.clone.sunk | while | flops 440975 | bytes 132278912 | solution.py:1333
  348.2 35.1 %decode.1 = (f32[8,128]{1,0:T(8,128)}, f32[72,128]{1,0:T(8,128)}) custom-call(bf16[1920,256]{1,0:T(8,128)(2,1)} %pad_select_fusion.points_ref, s32[1920,1]{1,0:T(8,128)} %reshape.334.count_ref, f32[8,128]{1,0:T(8,128)} %reduce_sum.99.stats_ref, f32[8,1152]{1,0:T(8,128)} %tile.27.kernel_ref, f32[8,1152]{1,0:T(8,128)} %tile.58.gain_ref, ...), custom_call_target="tpu_custom_call" | custom-call | flops 35 | bytes 105000000 | tf_op jit(solution)/shard_map/decode/pallas_call | solution.py:888
  384.8 18.7 %all-to-all-start.9 = ((f32[32,1,352]{2,1,0:T(1,128)}), f32[32,1,352]{2,1,0:T(1,128)S(1)}, u32[]{:S(2)}, u32[]{:S(2)}) async-start(f32[32,1,352]{2,1,0:T(1,128)} %broadcast_in_dim_reshape.4), calls=%async_computation.9 | async-start | bytes 98304 | tf_op jit(solution)/shard_map/all_to_all | solution.py:1342
  403.5 7.3 %all-to-all-done.9 = f32[32,1,352]{2,1,0:T(1,128)S(1)} async-done(((f32[32,1,352]{2,1,0:T(1,128)}), f32[32,1,352]{2,1,0:T(1,128)S(1)}, u32[]{:S(2)}, u32[]{:S(2)}) %all-to-all-start.9) | async-done | bytes 45088 | tf_op jit(solution)/shard_map/all_to_all | solution.py:1342
  411.5 2.6 all-to-all-start.10
  415.1 6.3 %all-to-all-done.10 = f32[32,1,352]{2,1,0:T(1,128)S(1)} async-done(((f32[32,1,352]{2,1,0:T(1,128)}), f32[32,1,352]{2,1,0:T(1,128)S(1)}, u32[]{:S(2)}, u32[]{:S(2)}) %all-to-all-start.10) | async-done | bytes 45088 | tf_op jit(solution)/shard_map/all_to_all | solution.py:1048
  434.6 3.0 concatenate.114
  437.6 3.3 multiply_subtract_fusion
  (247 shorter events, 83.1 us)
Async XLA Ops:
  25.9 9.4 %copy-start.31 = (bf16[32]{0:T(256)(128)(2,1)S(1)}, bf16[32]{0:T(256)(128)(2,1)}, u32[]{:S(2)}) copy-start(bf16[32]{0:T(256)(128)(2,1)} %param.29) | copy-start | bytes 196
  27.7 15.7 %all-to-all-start.3 = ((f32[32,8,128]{2,1,0:T(8,128)}), f32[32,8,128]{2,1,0:T(8,128)S(1)}, u32[]{:S(2)}, u32[]{:S(2)}) async-start(f32[32,8,128]{2,1,0:T(8,128)} %broadcast_in_dim.141), calls=%async_computation.3 | async-start | bytes 262144 | tf_op jit(solution)/shard_map/all_to_all | solution.py:1048
  63.4 8.4 %copy-start.10 = (bf16[3,3,80,128]{3,2,1,0:T(8,128)(2,1)S(1)}, bf16[3,3,80,128]{3,2,1,0:T(8,128)(2,1)}, u32[]{:S(2)}) copy-start(bf16[3,3,80,128]{3,2,1,0:T(8,128)(2,1)} %param.27) | copy-start | bytes 552964
  69.1 7.3 %copy-start.37 = (bf16[144,128]{1,0:T(8,128)(2,1)S(1)}, bf16[144,128]{1,0:T(8,128)(2,1)}, u32[]{:S(2)}) copy-start(bf16[144,128]{1,0:T(8,128)(2,1)} %get-tuple-element.418) | copy-start | bytes 110596
  69.1 8.6 %collective-permute-start.4 = (bf16[144,128]{1,0:T(8,128)(2,1)}, bf16[144,128]{1,0:T(8,128)(2,1)S(1)}, u32[]{:S(2)}, u32[]{:S(2)}) collective-permute-start(bf16[144,128]{1,0:T(8,128)(2,1)} %get-tuple-element.417), channel_id=1, source_target_pairs={{0,4},{4,8},{8,12},{12,16},{16,20},{20,24},{24,28},{1,5},{5,9},{9,... | collective-permute-start | bytes 110600 | tf_op jit(solution)/shard_map/ppermute | solution.py:1180
  72.8 14.6 %all-to-all-start.5 = ((bf16[4,3,3,80,128]{4,3,2,1,0:T(8,128)(2,1)}), bf16[4,3,3,80,128]{4,3,2,1,0:T(8,128)(2,1)S(1)}, u32[]{:S(2)}, u32[]{:S(2)}) async-start(bf16[4,3,3,80,128]{4,3,2,1,0:T(8,128)(2,1)} %broadcast_in_dim.151), calls=%async_computation.5 | async-start | bytes 1474560 | tf_op jit(solution)/shard_map/all_to_all | solution.py:1048
  76.4 5.9 %collective-permute-start.5 = (bf16[144,128]{1,0:T(8,128)(2,1)S(1)}, bf16[144,128]{1,0:T(8,128)(2,1)S(1)}, u32[]{:S(2)}, u32[]{:S(2)}) collective-permute-start(bf16[144,128]{1,0:T(8,128)(2,1)S(1)} %copy-done.37), channel_id=1, source_target_pairs={{4,0},{8,4},{12,8},{16,12},{20,16},{24,20},{28,24},{5,1},{9,5},{13... | collective-permute-start | bytes 110600 | tf_op jit(solution)/shard_map/ppermute | solution.py:1179
  87.4 20.7 %all-to-all-start.4 = ((bf16[4,944,128]{2,1,0:T(8,128)(2,1)}), bf16[4,944,128]{2,1,0:T(8,128)(2,1)S(1)}, u32[]{:S(2)}, u32[]{:S(2)}) async-start(bf16[4,944,128]{2,1,0:T(8,128)(2,1)} %bitcast_dynamic-update-slice_fusion.4), calls=%async_computation.4 | async-start | bytes 1933312 | tf_op jit(solution)/shard_map/all_to_all | solution.py:1183
  91.0 191.1 %copy-start.19 = (s32[2]{0:T(128)}, s32[2]{0:T(128)S(1)}, u32[]{:S(2)}) copy-start(s32[2]{0:T(128)S(1)} %add_convert_fusion.1.edge_ref) | copy-start | bytes 28
  108.3 17.7 %copy-start.20 = (pred[4,944]{1,0:T(4,128)(4,1)}, pred[4,944]{1,0:T(4,128)(4,1)S(1)}, u32[]{:S(2)}) copy-start(pred[4,944]{1,0:T(4,128)(4,1)S(1)} %broadcast_compare_fusion.3) | copy-start | bytes 11332
  126.3 27.5 %copy-start = (f32[1920,128]{1,0:T(8,128)}, f32[1920,128]{1,0:T(8,128)S(1)}, u32[]{:S(2)}) copy-start(f32[1920,128]{1,0:T(8,128)S(1)} %get-tuple-element.902) | copy-start | bytes 2949124
  126.3 27.5 %copy-start.2 = (bf16[1920,128]{1,0:T(8,128)(2,1)}, bf16[1920,128]{1,0:T(8,128)(2,1)S(1)}, u32[]{:S(2)}) copy-start(bf16[1920,128]{1,0:T(8,128)(2,1)S(1)} %get-tuple-element.907) | copy-start | bytes 1474564
  126.3 27.5 %copy-start.4 = (s32[8,1920]{1,0:T(8,128)}, s32[8,1920]{1,0:T(8,128)S(1)}, u32[]{:S(2)}) copy-start(s32[8,1920]{1,0:T(8,128)S(1)} %get-tuple-element.914) | copy-start | bytes 184324
  127.4 26.4 %copy-start.33 = (f32[128]{0:T(128)S(1)}, f32[128]{0:T(128)}, u32[]{:S(2)}) copy-start(f32[128]{0:T(128)} %split.10) | copy-start | bytes 1540
  127.4 27.0 %copy-start.32 = (f32[16]{0:T(128)S(1)}, f32[16]{0:T(128)}, u32[]{:S(2)}) copy-start(f32[16]{0:T(128)} %split.11) | copy-start | bytes 196
  182.0 53.2 %all-to-all-start.6 = ((f32[32,96,128]{2,1,0:T(8,128)}), f32[32,96,128]{2,1,0:T(8,128)}, u32[]{:S(2)}, u32[]{:S(2)}) async-start(f32[32,96,128]{2,1,0:T(8,128)} %bitcast.176), calls=%async_computation.6 | async-start | bytes 3145728 | tf_op jit(solution)/shard_map/all_to_all | solution.py:1063
  186.1 6.3 %copy-start.22 = (f32[48,128]{1,0:T(8,128)S(1)}, f32[48,128]{1,0:T(8,128)}, u32[]{:S(2)}) copy-start(f32[48,128]{1,0:T(8,128)} %get-tuple-element.427) | copy-start | bytes 73732
  186.1 6.5 %copy-start.26 = (f32[32,128]{1,0:T(8,128)S(1)}, f32[32,128]{1,0:T(8,128)}, u32[]{:S(2)}) copy-start(f32[32,128]{1,0:T(8,128)} %get-tuple-element.429) | copy-start | bytes 49156
  186.2 162.0 %all-gather.5.cloned.1.call-start = ((), (), s32[]{:S(2)}) async-start(), calls=%async_computation.12 | async-start | bytes 1622016 | tf_op jit(solution)/shard_map/all_gather | solution.py:1309
  188.6 4.8 %collective-permute-start.6 = (bf16[352,128]{1,0:T(8,128)(2,1)S(1)}, bf16[352,128]{1,0:T(8,128)(2,1)S(1)}, u32[]{:S(2)}, u32[]{:S(2)}) collective-permute-start(bf16[352,128]{1,0:T(8,128)(2,1)S(1)} %copy-done.36), channel_id=1, source_target_pairs={{0,1},{1,2},{2,3},{3,4},{4,5},{5,6},{6,7},{7,8},{8,9},{9,10},{10,1... | collective-permute-start | bytes 270344 | tf_op jit(solution)/shard_map/ppermute | solution.py:1055
  190.7 4.3 collective-permute-start.7
  208.3 25.3 %copy-start.28 = (f32[8,384]{1,0:T(8,128)S(1)}, f32[8,384]{1,0:T(8,128)}, u32[]{:S(2)}) copy-start(f32[8,384]{1,0:T(8,128)} %get-tuple-element.428) | copy-start | bytes 36868
  237.4 72.5 %all-to-all-start.7 = ((f32[32,72,128]{2,1,0:T(8,128)}), f32[32,72,128]{2,1,0:T(8,128)}, u32[]{:S(2)}, u32[]{:S(2)}) async-start(f32[32,72,128]{2,1,0:T(8,128)} %bitcast.179), calls=%async_computation.7 | async-start | bytes 2359296 | tf_op jit(solution)/shard_map/all_to_all | solution.py:1063
  275.2 4.3 collective-permute-start.8
  277.3 4.8 %collective-permute-start.9 = (bf16[352,384]{1,0:T(8,128)(2,1)}, bf16[352,384]{1,0:T(8,128)(2,1)S(1)}, u32[]{:S(2)}, u32[]{:S(2)}) collective-permute-start(bf16[352,384]{1,0:T(8,128)(2,1)} %get-tuple-element.433), channel_id=1, source_target_pairs={{1,0},{2,1},{3,2},{4,3},{5,4},{6,5},{7,6},{8,7},{9,8},{10,9},{11,1... | collective-permute-start | bytes 811016 | tf_op jit(solution)/shard_map/ppermute | solution.py:1055
  309.9 13.7 %copy-start.15 = (s32[1888]{0:T(1024)S(1)}, s32[1888]{0:T(1024)}, u32[]{:S(2)}) copy-start(s32[1888]{0:T(1024)} %copy-done.14) | copy-start | bytes 22660
  311.8 22.4 %all-to-all-start.8 = ((bf16[4,768,128]{2,1,0:T(8,128)(2,1)}), bf16[4,768,128]{2,1,0:T(8,128)(2,1)}, u32[]{:S(2)}, u32[]{:S(2)}) async-start(bf16[4,768,128]{2,1,0:T(8,128)(2,1)} %bitcast.192), calls=%async_computation.8 | async-start | bytes 1572864 | tf_op jit(solution)/shard_map/all_to_all | solution.py:1319
  322.4 105.6 %all-gather.3.cloned.1.call-start = ((), (), s32[]{:S(2)}) async-start(), calls=%async_computation.11 | async-start | bytes 1216512 | tf_op jit(solution)/shard_map/all_gather | solution.py:1326
  348.2 35.1 %copy-start.24 = (f32[8,128]{1,0:T(8,128)S(1)}, f32[8,128]{1,0:T(8,128)}, u32[]{:S(2)}) copy-start(f32[8,128]{1,0:T(8,128)} %get-tuple-element.580) | copy-start | bytes 12292
  348.2 65.9 %copy-start.5 = (f32[3072,128]{1,0:T(8,128)S(1)}, f32[3072,128]{1,0:T(8,128)}, u32[]{:S(2)}) copy-start(f32[3072,128]{1,0:T(8,128)} %all-gather.5.cloned.1.call-done) | copy-start | bytes 4718596
  384.8 26.1 %all-to-all-start.9 = ((f32[32,1,352]{2,1,0:T(1,128)}), f32[32,1,352]{2,1,0:T(1,128)S(1)}, u32[]{:S(2)}, u32[]{:S(2)}) async-start(f32[32,1,352]{2,1,0:T(1,128)} %broadcast_in_dim_reshape.4), calls=%async_computation.9 | async-start | bytes 98304 | tf_op jit(solution)/shard_map/all_to_all | solution.py:1342
  411.5 9.9 %all-to-all-start.10 = ((f32[32,1,352]{2,1,0:T(1,128)}), f32[32,1,352]{2,1,0:T(1,128)S(1)}, u32[]{:S(2)}, u32[]{:S(2)}) async-start(f32[32,1,352]{2,1,0:T(1,128)} %broadcast_in_dim.158), calls=%async_computation.10 | async-start | bytes 98304 | tf_op jit(solution)/shard_map/all_to_all | solution.py:1048
  (21 other events, 35.0 us)
Sparse Core Ops, SparseCore 0:
  237.5 86.4 all-gather.4
  326.9 68.9 all-gather.2

commit v2 on v1

--- a/solution.py
+++ b/solution.py
@@ -15,7 +15,7 @@
 CHUNK = 384
 CAP = 768
 EDGE_CAP = 128
-LARGE_ROWS = 2304
+EMPTY = -1e30
 FOCAL_ALPHA = 0.25
 BN_EPSILON = 0.001
 CLIP_LIMIT = 0.05
@@ -120,8 +120,14 @@
     )(*((index, feats) if fresh else (index, feats, old)))
 
 
-def middle_kernel(columns, edge_ref, grid_ref, weight_ref, bias_ref, out_ref):
+def middle_kernel(columns, edge_ref, grid_ref, kernel_ref, bias_ref, out_ref, weight_ref):
     low = low_lanes(columns)
+    none = jnp.zeros((LANES, LANES // 2), BF16)
+    for place in range(9):
+        one, two, three = (kernel_ref[place * 3 + e] for e in range(3))
+        rows = slice(place * LANES, (place + 1) * LANES)
+        weight_ref[0, rows, :] = jnp.concatenate([one, two, three, none], axis=1)
+        weight_ref[1, rows, :] = jnp.concatenate([two, one, none, three], axis=1)
     grid_rows = BLOCK_ROWS + 2 * HALO
     depth_out = DEPTH // 2
 
@@ -163,25 +169,17 @@
     lax.fori_loop(0, BLOCK_ROWS + 2, row, 0)
 
 
-def middle_weights(w_mid):
-    c_mid = w_mid.shape[4]
-    kernel = w_mid.transpose(0, 1, 3, 2, 4).reshape(-1, 3, c_mid)
-    none = jnp.zeros_like(kernel[:, 0])
-    even = jnp.concatenate([kernel[:, 0], kernel[:, 1], kernel[:, 2], none], axis=1)
-    odd = jnp.concatenate([kernel[:, 1], kernel[:, 0], none, kernel[:, 2]], axis=1)
-    return jnp.stack([even, odd])
-
-
-def middle_forward(edges, grid, weights, bias, columns):
+def middle_forward(edges, grid, w_mid, bias, columns):
     return pl.pallas_call(
         functools.partial(middle_kernel, columns),
         out_shape=jax.ShapeDtypeStruct(((BLOCK_ROWS + 2) * columns, PAIRS * LANES), BF16),
         in_specs=smem(1) + vmem(3),
         out_specs=vmem(1)[0],
+        scratch_shapes=[pltpu.VMEM((2, 9 * LANES, 2 * LANES), BF16)],
         compiler_params=params(),
         cost_estimate=work(26),
         name="middle_forward",
-    )(edges, grid, weights, jnp.tile(bias.reshape(1, -1), (8, 2)))
+    )(edges, grid, w_mid, jnp.tile(bias.reshape(1, -1), (8, 2)))
 
 
 def column_taps(own, j):
@@ -194,12 +192,22 @@
 
 
 def middle_data_kernel(
-    count, columns, index_ref, edge_ref, d_ref, above_ref, below_ref, weight_ref, out_ref,
-    near, far, wide, rows,
+    count, columns, index_ref, edge_ref, d_ref, above_ref, below_ref, kernel_ref, out_ref,
+    near, far, wide, rows, weight_ref,
 ):
     padded = BLOCK_ROWS + 2
     half = LANES // 2
     cells = DEPTH * BLOCK_ROWS * columns
+    span = 10 * half
+    for a, first, side in ((1, 0, 0), (2, 0, 1), (0, span, 1)):
+        lanes = slice(side * LANES, (side + 1) * LANES)
+        for b in range(3):
+            for e in range(3):
+                block = (2 - b) * 2 + e if e < 2 else 6 + 2 - b
+                turned = kernel_ref[(a * 3 + b) * 3 + e].astype(F32).T.astype(BF16)
+                weight_ref[first + block * half : first + (block + 1) * half, lanes] = turned
+        weight_ref[first + span - half : first + span, lanes] = jnp.zeros((half, LANES), BF16)
+    weight_ref[span:, :LANES] = jnp.zeros((span, LANES), BF16)
 
     def build(r, source, place, factor):
         for j in range(PAIRS):
@@ -249,23 +257,7 @@
     out_ref[...] = rows[...].astype(BF16)
 
 
-def middle_data_weights(w_mid):
-    three, _, _, c_in, c_out = w_mid.shape
-    turned = w_mid.transpose(0, 1, 2, 4, 3)[:, ::-1]
-    near = turned[:, :, :2].reshape(three, -1, c_in)
-    far = turned[:, :, 2].reshape(three, -1, c_in)
-    block = jnp.concatenate([near, far, jnp.zeros((three, c_out, c_in), w_mid.dtype)], axis=1)
-    none = jnp.zeros_like(block[0])
-    return jnp.concatenate(
-        [
-            jnp.concatenate([block[1], none], axis=0),
-            jnp.concatenate([block[2], block[0]], axis=0),
-        ],
-        axis=1,
-    )
-
-
-def middle_data(index, edges, d_rows, above, below, weights, columns):
+def middle_data(index, edges, d_rows, above, below, w_mid, columns):
     count = index.shape[0]
     padded = (BLOCK_ROWS + 2) * columns
     return pl.pallas_call(
@@ -278,11 +270,12 @@
             pltpu.VMEM((DEPTH // 2, padded, LANES), BF16),
             pltpu.VMEM((DEPTH * BLOCK_ROWS * columns + 8, LANES), F32),
             pltpu.VMEM((count, LANES), F32),
+            pltpu.VMEM((10 * LANES, 2 * LANES), BF16),
         ],
         compiler_params=params(),
         cost_estimate=work(30),
         name="middle_data",
-    )(index, edges, d_rows, above, below, weights)
+    )(index, edges, d_rows, above, below, w_mid)
 
 
 def middle_weight_kernel(columns, grid_ref, d_ref, out_ref, total, taps_ref, turned):
@@ -327,8 +320,6 @@
 
     lax.fori_loop(0, BLOCK_ROWS // 2, rows, 0)
     low = low_lanes(LANES // 2)
-    used = 27 * half
-    out_ref[used:, :] = jnp.zeros((out_ref.shape[0] - used, LANES), F32)
     for place in range(9):
         for side in range(2):
             turned[...] = total[
@@ -344,10 +335,10 @@
                 )
 
 
-def middle_weight(grid, d_rows, columns, total_rows):
+def middle_weight(grid, d_rows, columns):
     return pl.pallas_call(
         functools.partial(middle_weight_kernel, columns),
-        out_shape=jax.ShapeDtypeStruct((total_rows, LANES), F32),
+        out_shape=jax.ShapeDtypeStruct((27 * LANES // 2, LANES), F32),
         in_specs=vmem(2),
         out_specs=vmem(1)[0],
         scratch_shapes=[
@@ -579,8 +570,6 @@
 
     lax.fori_loop(0, rows // 2, two, 0)
     share = half // blocks
-    used = 9 * depth_out * half
-    out_ref[used:, :] = jnp.zeros((out_ref.shape[0] - used, LANES), F32)
     for b in range(3):
         for e in range(3):
             for j in range(PAIRS):
@@ -595,11 +584,11 @@
                         ]
 
 
-def region_weight(d_own, bev, columns, blocks, total_rows):
+def region_weight(d_own, bev, columns, blocks):
     width = PAIRS * LANES
     return pl.pallas_call(
         functools.partial(region_weight_kernel, columns, blocks),
-        out_shape=jax.ShapeDtypeStruct((total_rows, LANES), F32),
+        out_shape=jax.ShapeDtypeStruct((9 * (DEPTH // 2) * (LANES // 2), LANES), F32),
         in_specs=vmem(2),
         out_specs=vmem(1)[0],
         scratch_shapes=[
@@ -731,7 +720,14 @@
 
 def second_tail(pooled):
     lane = lax.broadcasted_iota(jnp.int32, pooled.shape, 1)
-    return jnp.where(lane < 32, pooled, jnp.where(lane == 32, 1.0, 0.0)).astype(BF16)
+    return jnp.where(lane < 32, pooled, jnp.where(lane == 32, 1.0, 0.0))
+
+
+def group_left(low, tail, count, g):
+    lane = lax.broadcasted_iota(jnp.int32, tail.shape, 1)
+    marked = (lane > 32) & (lane < 37) & (lane - (33 - 4 * g) >= count)
+    side = jnp.where(marked, 1.0, tail).astype(BF16)
+    return jnp.concatenate([low[:, g * LANES : (g + 1) * LANES], side], axis=1)
 
 
 def encode_kernel(
@@ -749,11 +745,11 @@
     low = act.astype(BF16)
     top = jnp.full((CHUNK, LANES), -jnp.inf, F32)
     for g in range(lanes // LANES):
-        left = jnp.concatenate([low[:, g * LANES : (g + 1) * LANES], tail], axis=1)
+        left = group_left(low, tail, count, g)
         part = jnp.dot(left, second_ref[...], preferred_element_type=F32)
         for s in range(min(4, slots - 4 * g)):
             p = 4 * g + s
-            one = jnp.where(p < count, part[:, s * LANES : (s + 1) * LANES], -jnp.inf)
+            one = part[:, s * LANES : (s + 1) * LANES]
             held[p] = one
             top = jnp.maximum(top, one)
     ties = jnp.zeros((CHUNK, LANES), F32)
@@ -820,13 +816,13 @@
     d_feat = d_feat_ref[...] * share_ref[...]
     d_tail = jnp.zeros((CHUNK, LANES), F32)
     for g in range(lanes // LANES):
-        left = jnp.concatenate([low[:, g * LANES : (g + 1) * LANES], tail], axis=1)
+        left = group_left(low, tail, count, g)
         part = jnp.dot(left, second_ref[...], preferred_element_type=F32)
         pieces = []
         for s in range(4):
             p = 4 * g + s
             if p < slots:
-                hit = (part[:, s * LANES : (s + 1) * LANES] == top) & (p < count)
+                hit = part[:, s * LANES : (s + 1) * LANES] == top
                 pieces.append(jnp.where(hit, d_feat, 0.0).astype(BF16))
             else:
                 pieces.append(jnp.zeros((CHUNK, LANES), BF16))
@@ -935,8 +931,9 @@
         row_two // c_one == col_two // c_two, jnp.tile(w_two[:c_one], (4, 4)), jnp.zeros((), BF16)
     )
     lower = jnp.concatenate([w_two[c_one:], bias_two.reshape(1, -1)], axis=0)
-    lower = jnp.pad(lower, ((0, LANES - lower.shape[0]), (0, 0)))
-    second = jnp.concatenate([upper, jnp.tile(lower, (1, 4))], axis=0)
+    lower = jnp.tile(jnp.pad(lower, ((0, LANES - lower.shape[0]), (0, 0))), (1, 4))
+    lower = jnp.where(row_two == c_one + 1 + col_two // c_two, jnp.asarray(EMPTY, BF16), lower)
+    second = jnp.concatenate([upper, lower], axis=0)
     kernel = jnp.pad(w_one.astype(F32), ((0, 1), (0, 0)))
     kernel = jnp.tile(kernel, (1, lanes // c_one))
     rows = jnp.pad(jnp.stack([gain, shift]).astype(F32), ((0, 6), (0, 0)))
@@ -1040,6 +1037,37 @@
     )(stats, kernel, gain, sums)
 
 
+def pack_kernel(plan, tiles, chunk, region_ref, middle_ref, tail_ref, out_ref, held):
+    sources = {"region": region_ref, "middle": middle_ref, "tail": tail_ref}
+    lane = lax.broadcasted_iota(jnp.int32, (1, LANES), 1)
+    for a, pieces in enumerate(plan):
+        at = 0
+        for name, low, high in pieces:
+            begin, end = low // LANES, -(-high // LANES)
+            held[at : at + end - begin, :] = sources[name][begin:end, :]
+            if low % LANES:
+                held[at : at + 1, :] = jnp.where(lane < low % LANES, 0.0, held[at : at + 1, :])
+            at += end - begin
+            if high % LANES:
+                held[at - 1 : at, :] = jnp.where(lane < high % LANES, held[at - 1 : at, :], 0.0)
+        held[at:, :] = jnp.zeros((held.shape[0] - at, LANES), F32)
+        for t in range(tiles):
+            out_ref[t * len(plan) + a] = held[t * chunk : (t + 1) * chunk, :].astype(BF16)
+
+
+def pack(plan, tiles, chunk, region, middle, tail):
+    return pl.pallas_call(
+        functools.partial(pack_kernel, plan, tiles, chunk),
+        out_shape=jax.ShapeDtypeStruct((tiles * len(plan), chunk, LANES), BF16),
+        in_specs=vmem(3),
+        out_specs=vmem(1)[0],
+        scratch_shapes=[pltpu.VMEM((tiles * chunk, LANES), F32)],
+        compiler_params=params(),
+        cost_estimate=work(3),
+        name="pack",
+    )(region, middle, tail)
+
+
 def everyone(values, axes):
     count = 1
     for axis in axes:
@@ -1053,14 +1081,6 @@
     count = lax.axis_size("tile") * lax.axis_size("anc")
     down = [(i, i + 1) for i in range(count - 1)]
     return lax.ppermute(last, axes, down), lax.ppermute(first, axes, [(j, i) for i, j in down])
-
-
-def sum_chunk(rows, axes):
-    devices = 1
-    for axis in axes:
-        devices *= lax.axis_size(axis)
-    parts = rows.reshape(devices, -1, rows.shape[1])
-    return jnp.sum(lax.all_to_all(parts, axes, 0, 0), axis=0)
 
 
 def shard_windows(segments, shard, count):
@@ -1136,6 +1156,7 @@
     exists = (jnp.arange(padded) < voxels).astype(jnp.int32)
     lines = jnp.pad(jnp.stack([layer, row, column, exists]), ((0, 4), (0, 0)))
     tile_edges = jnp.stack([joined(tile * tile_rows), joined((tile + 1) * tile_rows)])
+    parts = everyone(w_rpn, ("anc",))
     stats, place = prepare(
         tile_edges.astype(jnp.int32),
         flat_points,
@@ -1146,11 +1167,10 @@
         device_rows,
         slots,
     )
-    sent, w_mid, w_rpn = lax.optimization_barrier((stats, w_mid, w_rpn))
+    sent, parts = lax.optimization_barrier((stats, parts))
     gathered = everyone(sent, both)
-    weights = middle_weights(w_mid)
-    data_weights = middle_data_weights(w_mid)
-    region = everyone(w_rpn, ("anc",)).transpose(1, 2, 0, 3, 4)
+    middle_kernel_all = w_mid.reshape(-1, c_vox, c_mid)
+    region = parts.transpose(1, 2, 0, 3, 4)
     region = region_order(region.reshape(w_rpn.shape[:2] + (-1, c_rpn)))
     stats = jnp.sum(gathered, axis=0)
     count_pos = stats[1, 8]
@@ -1227,7 +1247,7 @@
     for k in range(blocks):
         top = first_row + k * BLOCK_ROWS
         edges.append(jnp.stack([joined(top), joined(top + BLOCK_ROWS)]).astype(jnp.int32))
-        bevs.append(middle_forward(edges[k], grids[k], weights, bias_mid, columns))
+        bevs.append(middle_forward(edges[k], grids[k], middle_kernel_all, bias_mid, columns))
 
     lanes = region.shape[2]
     region_in = region.transpose(0, 2, 1, 3).reshape(3 * lanes, 3 * c_rpn)
@@ -1261,15 +1281,13 @@
         above, below = neighbour_rows(firsts[0], lasts[-1])
         return [above] + lasts[:-1], firsts[1:] + [below]
 
-    devices = anc_count * tile_count
-    unit = devices * 8
     above, below = beside(d_first, d_last)
-    region_rows = -(-(9 * w_rpn.shape[2] * anc_count) // unit) * unit
     grad_region = sum(
-        region_weight(d_rows[k], bevs[k], columns, anc_count, region_rows) for k in range(blocks)
-    )
-    d_rows, grad_region = lax.optimization_barrier((d_rows, grad_region))
-    region_chunk = sum_chunk(grad_region, both)
+        region_weight(d_rows[k], bevs[k], columns, anc_count) for k in range(blocks)
+    )
+    d_rows, grad_region, above, below = lax.optimization_barrier(
+        (d_rows, grad_region, above, below)
+    )
     d_mids, mid_sums = [], 0.0
     mid_first, mid_last = [], []
     for k in range(blocks):
@@ -1281,13 +1299,8 @@
         mid_last.append(end_row)
         mid_sums = mid_sums + sums
     above, below = beside(mid_first, mid_last)
-    middle_size = w_mid.size
-    tail_size = c_rpn * outs + bn_gain.shape[0] + biases.shape[0]
-    used = middle_size // LANES
-    middle_rows = -(-max(used - (-tail_size // LANES), LARGE_ROWS) // unit) * unit
-    grad_mid = sum(
-        middle_weight(grids[k], d_mids[k], columns, middle_rows) for k in range(blocks)
-    )
+    grad_mid = sum(middle_weight(grids[k], d_mids[k], columns) for k in range(blocks))
+    grad_mid, above, below = lax.optimization_barrier((grad_mid, above, below))
 
     head_three = head_sums.reshape(3, outs, c_rpn)
     grad_head = (head_three[0] + head_three[1] + head_three[2]).T
@@ -1303,15 +1316,25 @@
         ]
     )
     tail_rows = jnp.pad(tail, (0, -tail.shape[0] % LANES)).reshape(-1, LANES)
-    grad_mid = lax.dynamic_update_slice(grad_mid, tail_rows, (used, 0))
-    own_at, grad_mid, region_chunk = lax.optimization_barrier((own_at, grad_mid, region_chunk))
-    middle_chunk = sum_chunk(grad_mid, both)
-    region_full = lax.all_gather(region_chunk, both, axis=0, tiled=True)
+    shard = master.shape[0]
+    segments = (
+        ("region", grad_region.size),
+        ("encoder", w_vfe1.size + w_vfe2.size),
+        ("middle", grad_mid.size),
+        ("tail", tail.shape[0]),
+    )
+    windows = shard_windows(segments, shard, anc_count)
+    plan = tuple(tuple(p for p in pieces if p[0] != "encoder") for pieces in windows)
+    tallest = max(sum(-(-high // LANES) - low // LANES for _, low, high in p) for p in plan)
+    chunk_rows = -(-tallest // (16 * tile_count)) * 16
+    packed = pack(plan, tile_count, chunk_rows, grad_region, grad_mid, tail_rows)
+    own_at, packed = lax.optimization_barrier((own_at, packed))
+    chunk = jnp.sum(lax.all_to_all(packed, both, 0, 0).astype(F32), axis=0)
 
     def collect(number, own_index, chunk):
         lists = sum(
             middle_data(
-                own_index[k], edges[k], d_mids[k], above[k], below[k], data_weights, columns
+                own_index[k], edges[k], d_mids[k], above[k], below[k], middle_kernel_all, columns
             )
             for k in range(blocks)
         )
@@ -1322,25 +1345,35 @@
         where = jnp.where(known, owner * CAP + mine, -1).reshape(padded, 1)
         return spread_lists(back.reshape(-1, LANES), where), chunk
 
-    d_feat, middle_chunk = collect(0, own_at, middle_chunk)
-    middle_full = lax.all_gather(middle_chunk, both, axis=0, tiled=True)
+    d_feat, chunk = collect(0, own_at, chunk)
+    chunk_square = jnp.sum(chunk * chunk)
+    early = everyone(chunk, ("tile",)).reshape(-1)
 
     def collect_more(state):
         number, held = state
         _, _, index = exchange(number)
         return number + 1, held + collect(number, index, ())[0]
 
-    _, d_feat = lax.while_loop(more, collect_more, (jnp.int32(1), d_feat))
-    d_feat, region_full = lax.optimization_barrier((d_feat, region_full))
+    d_feat = lax.cond(
+        rounds > 1,
+        lambda held: lax.while_loop(more, collect_more, (jnp.int32(1), held))[1],
+        lambda held: held,
+        d_feat,
+    )
     first_sums, second_sums = decode(
         flat_points, counts, stats, kernel, gain_rows, first, second, feat, share, d_feat, slots
     )
 
     late = jnp.concatenate([first_sums, second_sums, row_sums[24:32]], axis=0)
     rows = late.shape[0]
-    late = late.reshape(devices, -1)
-    late = jnp.sum(lax.all_to_all(late[:, None], both, 0, 0), axis=0)
-    late = everyone(late, both).reshape(rows, LANES)
+    late, early = lax.optimization_barrier((late, early))
+    late = late.reshape(anc_count * tile_count, 1, -1)
+    late = jnp.sum(lax.all_to_all(late, both, 0, 0), axis=0)
+    size = late.shape[1]
+    late = jnp.concatenate([late, chunk_square.reshape(1, 1)], axis=1)
+    late = everyone(late, both)
+    square_sum = jnp.sum(late[:, 0, size])
+    late = late[:, 0, :size].reshape(rows, LANES)
     encoder = finish_encoder(stats, kernel, gain_rows, late[:8])
     second_total = late[8 : 8 + second_sums.shape[0]]
     loss = late[rows - 1, 0] / count_pos
@@ -1356,36 +1389,25 @@
             jnp.zeros((c_mid + c_rpn + outs,), F32),
         ]
     )
-    shard = master.shape[0]
-    segments = (
-        ("region", w_rpn.size * anc_count),
-        ("encoder", encoder_flat.shape[0]),
-        ("middle", middle_size),
-        ("tail", tail_size),
-    )
-    region_flat = region_full.reshape(-1)
-    middle_flat = middle_full.reshape(-1)
 
     def assemble(pieces):
-        parts = []
+        parts, at = [], 0
         for name, low, high in pieces:
             if name == "encoder":
                 parts.append(encoder_flat[low:high])
-            elif name == "region":
-                parts.append(region_flat[low:high])
-            elif name == "middle":
-                parts.append(middle_flat[low:high])
-            else:
-                early = middle_flat[middle_size + low : middle_size + high]
-                parts.append(early + tail_late[low:high])
+                continue
+            start = at + low % LANES
+            part = early[start : start + high - low]
+            at += (-(-high // LANES) - low // LANES) * LANES
+            parts.append(part + tail_late[low:high] if name == "tail" else part)
         return jnp.concatenate(parts) if len(parts) > 1 else parts[0]
 
     reduced = None
-    for a, pieces in enumerate(shard_windows(segments, shard, anc_count)):
+    for a, pieces in enumerate(windows):
         one = assemble(pieces)
         reduced = one if a == 0 else jnp.where(anc == a, one, reduced)
-    square_sum = jnp.sum(region_full * region_full) + jnp.sum(middle_full * middle_full)
-    square_sum = square_sum + jnp.sum(encoder_flat * encoder_flat) + jnp.sum(tail_late * tail_late)
+    square_sum = square_sum + jnp.sum(encoder_flat * encoder_flat)
+    square_sum = square_sum + jnp.sum(tail_late * tail_late)
     norm_value = jnp.sqrt(square_sum)
     clipped = reduced * jnp.minimum(1.0, CLIP_LIMIT / (norm_value + 1e-06))
     first_new = BETA_FIRST * moment1 + (1.0 - BETA_FIRST) * clipped

time: 457 us -> 389 us (0.85)
  starting transfers between devices: 94 us -> 60.5 us
  between operations: 22.8 us -> 8.82 us
  loops' own time: 7.82 us -> 0.19 us
  other arithmetic: 27.3 us -> 19.8 us
    all_to_all x3 -> x2, starting transfers between devices: 55.1 us -> 13.3 us  [the longest x1 8.19 us: on_device(): chunk = jnp.sum(lax.all_to_all(packed, both, 0, 0).astype(F32), axis=0)]
    ppermute x2, starting transfers between devices: 3.05 us -> 12.8 us  [neighbour_rows(): lax.ppermute(first, axes, [(j, i) for i, j in down])]
    another operation x1, loops' own time: 7.59 us -> 0.19 us  [on_device(): lax.cond(rounds > 1, lambda held: lax.while_loop(more, collect_more, (jnp...]
    all_to_all x1, starting transfers between devices: 10.6 us -> 4.19 us  [collect(): back = lax.all_to_all(lists.reshape(anc_count, CAP, LANES), 'anc', 0, 0)]
    slice x7 -> x4, local copies, waits for them, and re-layouts: 6.78 us -> 0.51 us  [the longest x3 0.38 us: assemble(): part = early[start:start + high - low]]
    pallas_call x1, Pallas kernels: 19.3 us -> 14.3 us  [encode(): pl.pallas_call(functools.partial(encode_kernel, slots), grid=(voxels // C...]
    all_to_all x3 -> x2, waiting for transfers between devices: 7.33 us -> 11.1 us  [the longest x1 6.7 us: on_device(): late = jnp.sum(lax.all_to_all(late, both, 0, 0), axis=0)]
    all_to_all x3 -> x4, starting transfers between devices: 13.6 us -> 16 us  [everyone(): return lax.all_to_all(copies, axes, 0, 0)]
  transfers between devices with their start and end apart: 16 -> 14, of which waited for: 8 -> 7; matrix products, arithmetic and copies ran while one was open for 10% -> 10% of each run, Pallas kernels for 24% -> 26%
where the time goes in v2:
time: 389 us; the launch traced here: 384 us
  Pallas kernels  202 us (52%)
  starting transfers between devices  60.5 us (16%)
  local copies, waits for them, and re-layouts  51.8 us (13%)
  waiting for transfers between devices  40.1 us (10%)
  other arithmetic  19.8 us (5%)
  between operations  8.82 us (2%)
    pallas_call x1, Pallas kernels, decode(): pl.pallas_call(functools.partial(decode_kernel, slots), grid=(voxels // C...  34.6 us
    pallas_call x1, Pallas kernels, middle_data(): pl.pallas_call(functools.partial(middle_data_kernel, count, columns), out...  27.5 us
    pallas_call x1, Pallas kernels, middle_forward(): pl.pallas_call(functools.partial(middle_kernel, columns), out_shape=jax.S...  26.3 us
    pallas_call x1, Pallas kernels, middle_weight(): pl.pallas_call(functools.partial(middle_weight_kernel, columns), out_shap...  25.2 us
    pallas_call x1, Pallas kernels, region_forward(): pl.pallas_call(functools.partial(region_kernel, columns), out_shape=(jax....  16.7 us
    all_to_all x4, waiting for transfers between devices, everyone(): return lax.all_to_all(copies, axes, 0, 0)  16.3 us
    all_to_all x4, starting transfers between devices, everyone(): return lax.all_to_all(copies, axes, 0, 0)  16 us
    pallas_call x1, Pallas kernels, scatter_rows(): pl.pallas_call(functools.partial(scatter_kernel, count, cells, fresh), ou...  15.3 us
  transfers between devices with their start and end apart: 14, of which 7 were waited for; matrix products, arithmetic and copies ran while one was open for 10% of the time, Pallas kernels for 26%

profile of v2, /device:TPU:0, one launch (start us, length us, event | category | flops | bytes accessed | tf_op | source)
XLA Modules:
  0.0 383.6 jit_solution(15324148200551999427)
XLA Ops:
  8.7 4.2 %all-to-all-start.3 = ((bf16[4,3,3,80,128]{4,3,2,1,0:T(8,128)(2,1)}), bf16[4,3,3,80,128]{4,3,2,1,0:T(8,128)(2,1)S(1)}, u32[]{:S(2)}, u32[]{:S(2)}) async-start(bf16[4,3,3,80,128]{4,3,2,1,0:T(8,128)(2,1)} %broadcast_in_dim.146), calls=%async_computation.3 | async-start | bytes 1474560 | tf_op jit(solution)/shard_map/all_to_all | solution.py:1076
  15.4 3.5 prepare.1
  20.8 3.2 all-to-all-done.3
  24.7 5.6 %all-to-all-start.4 = ((f32[32,8,128]{2,1,0:T(8,128)}), f32[32,8,128]{2,1,0:T(8,128)S(1)}, u32[]{:S(2)}, u32[]{:S(2)}) async-start(f32[32,8,128]{2,1,0:T(8,128)} %broadcast_in_dim.147), calls=%async_computation.4 | async-start | bytes 262144 | tf_op jit(solution)/shard_map/all_to_all | solution.py:1076
  32.3 6.2 %all-to-all-done.4 = f32[32,8,128]{2,1,0:T(8,128)S(1)} async-done(((f32[32,8,128]{2,1,0:T(8,128)}), f32[32,8,128]{2,1,0:T(8,128)S(1)}, u32[]{:S(2)}, u32[]{:S(2)}) %all-to-all-start.4) | async-done | bytes 131104 | tf_op jit(solution)/shard_map/all_to_all | solution.py:1076
  39.1 14.3 %encode.1 = (f32[1920,128]{1,0:T(8,128)S(1)}, f32[1920,128]{1,0:T(8,128)}) custom-call(bf16[1920,256]{1,0:T(8,128)(2,1)} %pad_select_fusion.points_ref, s32[1920,1]{1,0:T(8,128)} %reshape.318.count_ref, f32[8,128]{1,0:T(8,128)} %reduce_sum.92.stats_ref, f32[8,1152]{1,0:T(8,128)} %tile.27.kernel_ref, f32[8,1152]{1,0:T(8,128)} %tile.58.gain_ref, ...), custom_call_target="tpu_custom_call" | custom-call | flops 19 | bytes 57000000 | tf_op jit(solution)/shard_map/encode/pallas_call | solution.py:767
  53.9 5.3 %gather_lists.11 = (bf16[4,944,128]{2,1,0:T(8,128)(2,1)}, bf16[144,128]{1,0:T(8,128)(2,1)}, bf16[144,128]{1,0:T(8,128)(2,1)}) custom-call(s32[2]{0:T(128)} %broadcast_84_offset_ref.2.offset_ref, f32[1920,128]{1,0:T(8,128)S(1)} %get-tuple-element.887.feat_ref, bf16[1920,128]{1,0:T(8,128)(2,1)S(1)} %pad.72.digit_ref, s32[8,1920]{1,0:T(8,128)S(1)} %get-tuple-element.889.place_ref), custom_call_target="tpu_custom_call" | custom-call | flops 5 | bytes 15000000 | tf_op jit(solution)/shard_map/gather_lists/pallas_call | solution.py:973
  59.2 2.7 collective-permute-start.4
  68.0 3.9 %collective-permute-done.5 = bf16[144,128]{1,0:T(8,128)(2,1)S(1)} collective-permute-done((bf16[144,128]{1,0:T(8,128)(2,1)S(1)}, bf16[144,128]{1,0:T(8,128)(2,1)S(1)}, u32[]{:S(2)}, u32[]{:S(2)}) %collective-permute-start.5) | collective-permute-done | bytes 36896 | tf_op jit(solution)/shard_map/ppermute | solution.py:1199
  72.5 3.8 all-to-all-start.5
  95.6 15.3 %grid_scatter.6 = bf16[56320,128]{1,0:T(8,128)(2,1)} custom-call(s32[3776]{0:T(1024)} %fusion.30.refs_0_, bf16[3776,128]{1,0:T(8,128)(2,1)} %bitcast.163), custom_call_target="tpu_custom_call" | custom-call | flops 15 | bytes 45000000 | tf_op jit(solution)/shard_map/grid_scatter/pallas_call | solution.py:111
  112.1 26.3 %middle_forward.1.bev_ref = bf16[4928,384]{1,0:T(8,128)(2,1)} custom-call(s32[2]{0:T(128)S(1)} %add_convert_fusion.1.edge_ref, bf16[56320,128]{1,0:T(8,128)(2,1)} %get-tuple-element.469.grid_ref, bf16[27,128,64]{2,1,0:T(8,128)(2,1)S(1)} %bitcast.153, f32[8,128]{1,0:T(8,128)} %tile.67.bias_ref), custom_call_target="tpu_custom_call" | custom-call | flops 26 | bytes 78000000 | tf_op jit(solution)/shard_map/middle_forward/pallas_call | solution.py:173
  139.7 16.7 %region_forward.1 = (bf16[4224,128]{1,0:T(8,128)(2,1)}, bf16[352,128]{1,0:T(8,128)(2,1)}, bf16[352,128]{1,0:T(8,128)(2,1)}, f32[48,128]{1,0:T(8,128)}, f32[32,128]{1,0:T(8,128)}) custom-call(f32[1,1]{1,0:T(1,128)S(6)} %div.125.scale_ref, bf16[4928,384]{1,0:T(8,128)(2,1)} %middle_forward.1.bev_ref, bf16[1152,384]{1,0:T(8,128)(2,1)} %bitcast.168, ...), custom_call_target="tpu_custom_call" | custom-call | flops 16 | bytes 48000000 | tf_op jit(solution)/shard_map/region_forward/pallas_call | solution.py:449
  160.9 10.3 %region_weight.1.region_ref = f32[2880,128]{1,0:T(8,128)} custom-call(bf16[4224,128]{1,0:T(8,128)(2,1)} %get-tuple-element.475.d_ref, bf16[4928,384]{1,0:T(8,128)(2,1)} %middle_forward.1.bev_ref), custom_call_target="tpu_custom_call" | custom-call | flops 10 | bytes 30000000 | tf_op jit(solution)/shard_map/region_weight/pallas_call | solution.py:589
  171.8 12.7 %region_data.1 = (bf16[4224,384]{1,0:T(8,128)(2,1)S(1)}, bf16[352,384]{1,0:T(8,128)(2,1)}, bf16[352,384]{1,0:T(8,128)(2,1)}, f32[8,384]{1,0:T(8,128)}) custom-call(s32[2]{0:T(128)S(1)} %add_convert_fusion.1.edge_ref, bf16[4224,128]{1,0:T(8,128)(2,1)} %get-tuple-element.475.d_ref, bf16[352,128]{1,0:T(8,128)(2,1)} %copy-done.16, bf16[352,128]{1,0:T(8,128)(2,1)} %copy-done.17, ...), custom_call_target="tpu_custom_call" | custom-call | flops 13 | bytes 39000000 | tf_op jit(solution)/shard_map/region_data/pallas_call | solution.py:528
  184.5 4.1 %collective-permute-start.8 = (bf16[352,384]{1,0:T(8,128)(2,1)}, bf16[352,384]{1,0:T(8,128)(2,1)S(1)}, u32[]{:S(2)}, u32[]{:S(2)}) collective-permute-start(bf16[352,384]{1,0:T(8,128)(2,1)} %get-tuple-element.479), channel_id=1, source_target_pairs={{0,1},{1,2},{2,3},{3,4},{4,5},{5,6},{6,7},{7,8},{8,9},{9,10},{10,1... | collective-permute-start | bytes 811016 | tf_op jit(solution)/shard_map/ppermute | solution.py:1083
  188.7 11.5 %collective-permute-start.9 = (bf16[352,384]{1,0:T(8,128)(2,1)}, bf16[352,384]{1,0:T(8,128)(2,1)}, u32[]{:S(2)}, u32[]{:S(2)}) collective-permute-start(bf16[352,384]{1,0:T(8,128)(2,1)} %get-tuple-element.480), channel_id=1, source_target_pairs={{1,0},{2,1},{3,2},{4,3},{5,4},{6,5},{7,6},{8,7},{9,8},{10,9},{11,1... | collective-permute-start | bytes 811016 | tf_op jit(solution)/shard_map/ppermute | solution.py:1083
  204.9 25.2 %middle_weight.1.middle_ref = f32[1728,128]{1,0:T(8,128)} custom-call(bf16[56320,128]{1,0:T(8,128)(2,1)} %get-tuple-element.469.grid_ref, bf16[4224,384]{1,0:T(8,128)(2,1)S(1)} %get-tuple-element.478.d_ref), custom_call_target="tpu_custom_call" | custom-call | flops 26 | bytes 78000000 | tf_op jit(solution)/shard_map/middle_weight/pallas_call | solution.py:339
  232.1 3.0 pack.1
  235.1 8.2 %all-to-all-start.6 = ((bf16[32,160,128]{2,1,0:T(8,128)(2,1)}), bf16[32,160,128]{2,1,0:T(8,128)(2,1)}, u32[]{:S(2)}, u32[]{:S(2)}) async-start(bf16[32,160,128]{2,1,0:T(8,128)(2,1)} %pack.1), calls=%async_computation.6 | async-start | bytes 2621440 | tf_op jit(solution)/shard_map/all_to_all | solution.py:1332
  243.3 27.5 %middle_data.6 = bf16[3072,128]{1,0:T(8,128)(2,1)} custom-call(s32[3072]{0:T(1024)} %reshape.293.index_ref, s32[2]{0:T(128)S(1)} %add_convert_fusion.1.edge_ref, bf16[4224,384]{1,0:T(8,128)(2,1)S(1)} %get-tuple-element.478.d_ref, bf16[352,384]{1,0:T(8,128)(2,1)S(1)} %collective-permute-done.8.above_ref, bf16[352,384]{1,0:T(8,128)(2,1)} %collective-permute-done.9.below_ref, ...), custom_call_target="tpu_custom_call" | custom-call | flops 30 | bytes 90000000 | tf_op jit(solution)/shard_map/middle_data/pallas_call | solution.py:263
  270.7 4.4 %all-to-all-done.6 = bf16[32,160,128]{2,1,0:T(8,128)(2,1)} async-done(((bf16[32,160,128]{2,1,0:T(8,128)(2,1)}), bf16[32,160,128]{2,1,0:T(8,128)(2,1)}, u32[]{:S(2)}, u32[]{:S(2)}) %all-to-all-start.6) | async-done | bytes 1310752 | tf_op jit(solution)/shard_map/all_to_all | solution.py:1332
  277.3 4.2 %all-to-all-start.7 = ((bf16[4,768,128]{2,1,0:T(8,128)(2,1)}), bf16[4,768,128]{2,1,0:T(8,128)(2,1)}, u32[]{:S(2)}, u32[]{:S(2)}) async-start(bf16[4,768,128]{2,1,0:T(8,128)(2,1)} %bitcast.169), calls=%async_computation.7 | async-start | bytes 1572864 | tf_op jit(solution)/shard_map/all_to_all | solution.py:1342
  284.5 8.7 %all-to-all-done.7 = bf16[4,768,128]{2,1,0:T(8,128)(2,1)} async-done(((bf16[4,768,128]{2,1,0:T(8,128)(2,1)}), bf16[4,768,128]{2,1,0:T(8,128)(2,1)}, u32[]{:S(2)}, u32[]{:S(2)}) %all-to-all-start.7) | async-done | bytes 786464 | tf_op jit(solution)/shard_map/all_to_all | solution.py:1342
  293.2 6.4 %spread_lists.6 = f32[1920,128]{1,0:T(8,128)} custom-call(bf16[3072,128]{1,0:T(8,128)(2,1)} %bitcast.47.received_ref, s32[1920,1]{1,0:T(8,128)} %reshape.319.where_ref), custom_call_target="tpu_custom_call" | custom-call | flops 6 | bytes 18000000 | tf_op jit(solution)/shard_map/spread_lists/pallas_call | solution.py:998
  301.7 3.6 all-to-all-start.8
  305.4 34.6 %decode.1 = (f32[8,128]{1,0:T(8,128)}, f32[72,128]{1,0:T(8,128)}) custom-call(bf16[1920,256]{1,0:T(8,128)(2,1)} %pad_select_fusion.points_ref, s32[1920,1]{1,0:T(8,128)} %reshape.318.count_ref, f32[8,128]{1,0:T(8,128)} %reduce_sum.92.stats_ref, f32[8,1152]{1,0:T(8,128)} %tile.27.kernel_ref, f32[8,1152]{1,0:T(8,128)} %tile.58.gain_ref, ...), custom_call_target="tpu_custom_call" | custom-call | flops 35 | bytes 105000000 | tf_op jit(solution)/shard_map/decode/pallas_call | solution.py:884
  341.5 5.1 %all-to-all-start.9 = ((f32[32,1,352]{2,1,0:T(1,128)}), f32[32,1,352]{2,1,0:T(1,128)S(1)}, u32[]{:S(2)}, u32[]{:S(2)}) async-start(f32[32,1,352]{2,1,0:T(1,128)} %reshape.320), calls=%async_computation.9 | async-start | bytes 98304 | tf_op jit(solution)/shard_map/all_to_all | solution.py:1371
  347.2 6.7 %all-to-all-done.9 = f32[32,1,352]{2,1,0:T(1,128)S(1)} async-done(((f32[32,1,352]{2,1,0:T(1,128)}), f32[32,1,352]{2,1,0:T(1,128)S(1)}, u32[]{:S(2)}, u32[]{:S(2)}) %all-to-all-start.9) | async-done | bytes 45088 | tf_op jit(solution)/shard_map/all_to_all | solution.py:1371
  358.4 6.9 %all-to-all-done.10 = f32[32,1,353]{2,1,0:T(1,128)S(1)} async-done(((f32[32,1,353]{2,1,0:T(1,128)}), f32[32,1,353]{2,1,0:T(1,128)S(1)}, u32[]{:S(2)}, u32[]{:S(2)}) %all-to-all-start.10) | async-done | bytes 45216 | tf_op jit(solution)/shard_map/all_to_all | solution.py:1076
  375.0 3.0 concatenate.94
  378.0 3.1 multiply_subtract_fusion
  (241 shorter events, 74.8 us)
Async XLA Ops:
  8.7 15.4 %all-to-all-start.3 = ((bf16[4,3,3,80,128]{4,3,2,1,0:T(8,128)(2,1)}), bf16[4,3,3,80,128]{4,3,2,1,0:T(8,128)(2,1)S(1)}, u32[]{:S(2)}, u32[]{:S(2)}) async-start(bf16[4,3,3,80,128]{4,3,2,1,0:T(8,128)(2,1)} %broadcast_in_dim.146), calls=%async_computation.3 | async-start | bytes 1474560 | tf_op jit(solution)/shard_map/all_to_all | solution.py:1076
  24.7 13.8 %all-to-all-start.4 = ((f32[32,8,128]{2,1,0:T(8,128)}), f32[32,8,128]{2,1,0:T(8,128)S(1)}, u32[]{:S(2)}, u32[]{:S(2)}) async-start(f32[32,8,128]{2,1,0:T(8,128)} %broadcast_in_dim.147), calls=%async_computation.4 | async-start | bytes 262144 | tf_op jit(solution)/shard_map/all_to_all | solution.py:1076
  32.3 30.3 %copy-start.45 = (f32[208]{0:T(256)}, f32[208]{0:T(256)S(1)}, u32[]{:S(2)}) copy-start(f32[208]{0:T(256)S(1)} %slice_convert_fusion.3) | copy-start | bytes 2500
  59.2 8.1 %collective-permute-start.4 = (bf16[144,128]{1,0:T(8,128)(2,1)}, bf16[144,128]{1,0:T(8,128)(2,1)S(1)}, u32[]{:S(2)}, u32[]{:S(2)}) collective-permute-start(bf16[144,128]{1,0:T(8,128)(2,1)} %get-tuple-element.467), channel_id=1, source_target_pairs={{0,4},{4,8},{8,12},{12,16},{16,20},{20,24},{24,28},{1,5},{5,9},{9,... | collective-permute-start | bytes 110600 | tf_op jit(solution)/shard_map/ppermute | solution.py:1200
  64.4 47.7 %copy-start.4 = (bf16[3,3,3,128,64]{4,3,2,1,0:T(8,128)(2,1)}, bf16[3,3,3,128,64]{4,3,2,1,0:T(8,128)(2,1)S(1)}, u32[]{:S(2)}) copy-start(bf16[3,3,3,128,64]{4,3,2,1,0:T(8,128)(2,1)S(1)} %copy.84) | copy-start | bytes 1327108
  66.0 5.8 %collective-permute-start.5 = (bf16[144,128]{1,0:T(8,128)(2,1)S(1)}, bf16[144,128]{1,0:T(8,128)(2,1)S(1)}, u32[]{:S(2)}, u32[]{:S(2)}) collective-permute-start(bf16[144,128]{1,0:T(8,128)(2,1)S(1)} %copy-done.43), channel_id=1, source_target_pairs={{4,0},{8,4},{12,8},{16,12},{20,16},{24,20},{28,24},{5,1},{9,5},{13... | collective-permute-start | bytes 110600 | tf_op jit(solution)/shard_map/ppermute | solution.py:1199
  72.5 20.4 %all-to-all-start.5 = ((bf16[4,944,128]{2,1,0:T(8,128)(2,1)}), bf16[4,944,128]{2,1,0:T(8,128)(2,1)S(1)}, u32[]{:S(2)}, u32[]{:S(2)}) async-start(bf16[4,944,128]{2,1,0:T(8,128)(2,1)} %bitcast_dynamic-update-slice_fusion.4), calls=%async_computation.5 | async-start | bytes 1933312 | tf_op jit(solution)/shard_map/all_to_all | solution.py:1203
  110.8 27.5 %copy-start = (f32[1920,128]{1,0:T(8,128)}, f32[1920,128]{1,0:T(8,128)S(1)}, u32[]{:S(2)}) copy-start(f32[1920,128]{1,0:T(8,128)S(1)} %get-tuple-element.921) | copy-start | bytes 2949124
  110.8 27.5 %copy-start.3 = (bf16[1920,128]{1,0:T(8,128)(2,1)}, bf16[1920,128]{1,0:T(8,128)(2,1)S(1)}, u32[]{:S(2)}) copy-start(bf16[1920,128]{1,0:T(8,128)(2,1)S(1)} %get-tuple-element.925) | copy-start | bytes 1474564
  110.9 27.5 %copy-start.6 = (s32[8,1920]{1,0:T(8,128)}, s32[8,1920]{1,0:T(8,128)S(1)}, u32[]{:S(2)}) copy-start(s32[8,1920]{1,0:T(8,128)S(1)} %get-tuple-element.932) | copy-start | bytes 184324
  112.1 26.3 %copy-start.41 = (f32[128]{0:T(128)S(1)}, f32[128]{0:T(128)}, u32[]{:S(2)}) copy-start(f32[128]{0:T(128)} %split.10) | copy-start | bytes 1540
  112.1 26.9 %copy-start.40 = (f32[16]{0:T(128)S(1)}, f32[16]{0:T(128)}, u32[]{:S(2)}) copy-start(f32[16]{0:T(128)} %split.11) | copy-start | bytes 196
  139.6 20.4 %copy-start.20 = (s32[4,944]{1,0:T(4,128)S(1)}, s32[4,944]{1,0:T(4,128)}, u32[]{:S(2)}) copy-start(s32[4,944]{1,0:T(4,128)} %get-tuple-element.560) | copy-start | bytes 45316
  139.6 20.4 %copy-start.21 = (s32[4,944]{1,0:T(4,128)S(1)}, s32[4,944]{1,0:T(4,128)}, u32[]{:S(2)}) copy-start(s32[4,944]{1,0:T(4,128)} %get-tuple-element.562) | copy-start | bytes 45316
  139.6 20.4 %copy-start.22 = (s32[4,944]{1,0:T(4,128)S(1)}, s32[4,944]{1,0:T(4,128)}, u32[]{:S(2)}) copy-start(s32[4,944]{1,0:T(4,128)} %get-tuple-element.603) | copy-start | bytes 45316
  139.6 20.4 %copy-start.24 = (s32[944]{0:T(1024)S(1)}, s32[944]{0:T(1024)}, u32[]{:S(2)}) copy-start(s32[944]{0:T(1024)} %copy-done.23) | copy-start | bytes 11332
  139.6 20.4 %copy-start.28 = (pred[4,944]{1,0:T(4,128)(4,1)S(1)}, pred[4,944]{1,0:T(4,128)(4,1)}, u32[]{:S(2)}) copy-start(pred[4,944]{1,0:T(4,128)(4,1)} %copy-done.27) | copy-start | bytes 11332
  139.7 20.4 %copy-start.33 = (pred[4,944]{1,0:T(4,128)(4,1)S(1)}, pred[4,944]{1,0:T(4,128)(4,1)}, u32[]{:S(2)}) copy-start(pred[4,944]{1,0:T(4,128)(4,1)} %get-tuple-element.561) | copy-start | bytes 11332
  156.3 14.8 %collective-permute-start.6 = (bf16[352,128]{1,0:T(8,128)(2,1)}, bf16[352,128]{1,0:T(8,128)(2,1)S(1)}, u32[]{:S(2)}, u32[]{:S(2)}) collective-permute-start(bf16[352,128]{1,0:T(8,128)(2,1)} %get-tuple-element.472), channel_id=1, source_target_pairs={{0,1},{1,2},{2,3},{3,4},{4,5},{5,6},{6,7},{7,8},{8,9},{9,10},{10,1... | collective-permute-start | bytes 270344 | tf_op jit(solution)/shard_map/ppermute | solution.py:1083
  158.7 12.4 %collective-permute-start.7 = (bf16[352,128]{1,0:T(8,128)(2,1)}, bf16[352,128]{1,0:T(8,128)(2,1)S(1)}, u32[]{:S(2)}, u32[]{:S(2)}) collective-permute-start(bf16[352,128]{1,0:T(8,128)(2,1)} %get-tuple-element.473), channel_id=1, source_target_pairs={{1,0},{2,1},{3,2},{4,3},{5,4},{6,5},{7,6},{8,7},{9,8},{10,9},{11,1... | collective-permute-start | bytes 270344 | tf_op jit(solution)/shard_map/ppermute | solution.py:1083
  171.8 28.3 %copy-start.32 = (f32[32,128]{1,0:T(8,128)S(1)}, f32[32,128]{1,0:T(8,128)}, u32[]{:S(2)}) copy-start(f32[32,128]{1,0:T(8,128)} %get-tuple-element.484) | copy-start | bytes 49156
  184.5 47.5 %collective-permute-start.8 = (bf16[352,384]{1,0:T(8,128)(2,1)}, bf16[352,384]{1,0:T(8,128)(2,1)S(1)}, u32[]{:S(2)}, u32[]{:S(2)}) collective-permute-start(bf16[352,384]{1,0:T(8,128)(2,1)} %get-tuple-element.479), channel_id=1, source_target_pairs={{0,1},{1,2},{2,3},{3,4},{4,5},{5,6},{6,7},{7,8},{8,9},{9,10},{10,1... | collective-permute-start | bytes 811016 | tf_op jit(solution)/shard_map/ppermute | solution.py:1083
  188.7 43.4 %collective-permute-start.9 = (bf16[352,384]{1,0:T(8,128)(2,1)}, bf16[352,384]{1,0:T(8,128)(2,1)}, u32[]{:S(2)}, u32[]{:S(2)}) collective-permute-start(bf16[352,384]{1,0:T(8,128)(2,1)} %get-tuple-element.480), channel_id=1, source_target_pairs={{1,0},{2,1},{3,2},{4,3},{5,4},{6,5},{7,6},{8,7},{9,8},{10,9},{11,1... | collective-permute-start | bytes 811016 | tf_op jit(solution)/shard_map/ppermute | solution.py:1083
  204.9 25.2 %copy-start.34 = (f32[8,384]{1,0:T(8,128)S(1)}, f32[8,384]{1,0:T(8,128)}, u32[]{:S(2)}) copy-start(f32[8,384]{1,0:T(8,128)} %get-tuple-element.483) | copy-start | bytes 36868
  204.9 25.8 %copy-start.38 = (f32[128]{0:T(128)S(1)}, f32[128]{0:T(128)}, u32[]{:S(2)}) copy-start(f32[128]{0:T(128)} %get-tuple-element.590) | copy-start | bytes 1540
  235.1 40.1 %all-to-all-start.6 = ((bf16[32,160,128]{2,1,0:T(8,128)(2,1)}), bf16[32,160,128]{2,1,0:T(8,128)(2,1)}, u32[]{:S(2)}, u32[]{:S(2)}) async-start(bf16[32,160,128]{2,1,0:T(8,128)(2,1)} %pack.1), calls=%async_computation.6 | async-start | bytes 2621440 | tf_op jit(solution)/shard_map/all_to_all | solution.py:1332
  277.3 15.9 %all-to-all-start.7 = ((bf16[4,768,128]{2,1,0:T(8,128)(2,1)}), bf16[4,768,128]{2,1,0:T(8,128)(2,1)}, u32[]{:S(2)}, u32[]{:S(2)}) async-start(bf16[4,768,128]{2,1,0:T(8,128)(2,1)} %bitcast.169), calls=%async_computation.7 | async-start | bytes 1572864 | tf_op jit(solution)/shard_map/all_to_all | solution.py:1342
  301.7 39.0 %all-to-all-start.8 = ((f32[8,160,128]{2,1,0:T(8,128)}), f32[8,160,128]{2,1,0:T(8,128)S(1)}, u32[]{:S(2)}, u32[]{:S(2)}) async-start(f32[8,160,128]{2,1,0:T(8,128)} %broadcast_in_dim.161), calls=%async_computation.8 | async-start | bytes 1310720 | tf_op jit(solution)/shard_map/all_to_all | solution.py:1076
  305.3 34.6 %copy-start.30 = (f32[8,128]{1,0:T(8,128)S(1)}, f32[8,128]{1,0:T(8,128)}, u32[]{:S(2)}) copy-start(f32[8,128]{1,0:T(8,128)} %get-tuple-element.589) | copy-start | bytes 12292
  305.4 41.2 %copy-start.10 = (f32[160,128]{1,0:T(8,128)S(1)}, f32[160,128]{1,0:T(8,128)}, u32[]{:S(2)}) copy-start(f32[160,128]{1,0:T(8,128)} %convert_reduce_fusion) | copy-start | bytes 245764
  341.5 12.4 %all-to-all-start.9 = ((f32[32,1,352]{2,1,0:T(1,128)}), f32[32,1,352]{2,1,0:T(1,128)S(1)}, u32[]{:S(2)}, u32[]{:S(2)}) async-start(f32[32,1,352]{2,1,0:T(1,128)} %reshape.320), calls=%async_computation.9 | async-start | bytes 98304 | tf_op jit(solution)/shard_map/all_to_all | solution.py:1371
  355.4 9.9 %all-to-all-start.10 = ((f32[32,1,353]{2,1,0:T(1,128)}), f32[32,1,353]{2,1,0:T(1,128)S(1)}, u32[]{:S(2)}, u32[]{:S(2)}) async-start(f32[32,1,353]{2,1,0:T(1,128)} %broadcast_in_dim.164), calls=%async_computation.10 | async-start | bytes 98304 | tf_op jit(solution)/shard_map/all_to_all | solution.py:1076
  (25 other events, 152.8 us)
